TPU v7x, 32 devices: a whole 2x2x4 slice. The times are simulated.
32 devices in a mesh: rep: 4 (over y, core), seq: 8 (over z, x).
Axes of the slice: x: 2, y: 2, z: 4, core: 2. Of those that a mesh axis runs over, the one named last changes fastest.
Arguments:
- tokens: float32 [4, 1024, 768], P('rep', 'seq'), may hold values from -6 to 6
- cotangent: float32 [4, 1024, 768], P('rep', 'seq'), may hold values from -6 to 6
- gain_attn: float32 [768], replicated, may hold values from 0.5 to 1.5
- gain_mlp: float32 [768], replicated, may hold values from 0.5 to 1.5
- w_qkv: float32 [768, 2304], P('seq'), may hold values from -0.21875 to 0.21875
- w_attn_out: float32 [768, 768], P('seq'), may hold values from -3 to 3
- router: float32 [768, 8], P('seq'), may hold values from -0.21875 to 0.21875
- rel_table: float32 [12, 32], replicated, may hold values from -4 to 4
- w_in: bfloat16 [8, 768, 3072], P('seq'), may hold values from -0.21875 to 0.21875
- w_out: bfloat16 [8, 3072, 768], P('seq'), may hold values from -0.109375 to 0.109375
- segment_ids: int32 [4, 1024], P('rep'), may hold values from 0 to 3, never falling along the last dimension, each value on 1 to 768 neighbouring positions
- expert_ids: int32 [4, 1024, 2], P('rep', 'seq'), may hold values from 0 to 7, all different within a row; in each aligned block of 128 rows (0 to 127, 128 to 255, ..., all dimensions but the last counted through in order) at most 64 rows name the same one
- rel_bucket: int32 [1024], replicated, may hold values from 0 to 31
Outputs:
- output: float32 [4, 1024, 768], P('rep', 'seq')
- input_grad: float32 [4, 1024, 768], P('rep', 'seq')
- grad_gain_attn: float32 [768], replicated
- grad_gain_mlp: float32 [768], replicated
- grad_w_qkv: float32 [768, 2304], P('seq')
- grad_w_attn_out: float32 [768, 768], P('seq')
- grad_router: float32 [768, 8], P('seq')
- grad_rel_table: float32 [12, 32], replicated
- grad_w_in: float32 [8, 768, 3072], P('seq', None, 'rep')
- grad_w_out: float32 [8, 3072, 768], P('seq', 'rep')
Inputs may be any that keep to these rules, and one draw needn't show every extreme that they name: `segment_ids`: segment numbers never fall along a sequence; each segment has 1 to 768 positions and one has exactly 768. `expert_ids`: the two experts of a token differ. Among the tokens of one device (aligned blocks of 128 positions) no expert is named more than 64 times, a bound that some block reaches.
All inputs are finite; a program needn't handle non-finite values.
Results may differ from a plain program's by a relative error of at most 0.015.
The roundings to bfloat16 on the way count: a program that leaves them out, or rounds other values in their place, can miss the bound.
Values may be sent and summed in bfloat16 or wider, within the bound.
No kernel may reach another device: no remote copies, remote signals or barrier semaphores. Data moves between devices by JAX's collectives and lax.ppermute only.
A program may use at most 320 MiB of HBM per device.

v0:
```python
from functools import partial
import math

import jax
import jax.numpy as jnp
from jax import lax
from jax.experimental import pallas as pl
from jax.experimental.pallas import tpu as pltpu
from jax.sharding import Mesh, PartitionSpec as P

D = 768
HEADS = 12
HEAD = 64
BUCKETS = 32
FF = 3072
GROUPS = 4
GHEADS = HEADS // GROUPS
GW = GHEADS * HEAD
EPS = 1e-06
HIGHEST = lax.Precision.HIGHEST
BF = jnp.bfloat16
F32 = jnp.float32
NT = (((1,), (1,)), ((), ()))
TN = (((0,), (0,)), ((), ()))
SEQ = ("g", "i")
REP = ("y", "c")


def dotf(a, b, dims=(((1,), (0,)), ((), ()))):
    return lax.dot_general(a, b, dims, preferred_element_type=F32)


def loop(count, body, init):
    if count <= 2:
        for step in range(count):
            init = body(step, init)
        return init
    return lax.fori_loop(0, count, body, init)


def ahead(block, own, count):
    return lax.rem(block + count - own, count)


def behind(step, own, count):
    return lax.rem(own + count - step, count)


def heads_apart(value, scale):
    lane = lax.broadcasted_iota(jnp.int32, value.shape, 1)
    value = value * jnp.asarray(scale, value.dtype)
    return jnp.concatenate(
        [jnp.where(lane // HEAD == head, value, jnp.zeros_like(value)) for head in range(GHEADS)],
        axis=0,
    )


def heads_beside(value, size):
    return jnp.concatenate(
        [value[head * size : (head + 1) * size] for head in range(GHEADS)], axis=1
    )


def turned(value):
    wide = jnp.concatenate((value, jnp.zeros((value.shape[0], -GW % 128), F32)), axis=1)
    return wide.T[:GW]


def turned_back(value):
    tall = jnp.concatenate((value, jnp.zeros((-GW % 128, value.shape[1]), F32)), axis=0)
    return tall.T[:, :GW]


def tile_mask(start, query_block, key_block, size):
    lane = lax.broadcasted_iota(jnp.int32, (size, size), 1)
    row = lax.broadcasted_iota(jnp.int32, (size, size), 0)
    allowed = (lane >= start - key_block * size) & (
        lane - row <= (query_block - key_block) * size
    )
    return jnp.where(allowed, 0.0, -1e30)


def bias_kernel(rows_ref, tiles_ref):
    heads, inner, count, size, _ = tiles_ref.shape

    def head_step(head, carry):
        for part in range(inner):
            tiles_ref[head, part, 0] = jnp.zeros((size, size), F32)
            for step in range(count - 1):
                gap = step * inner + part
                pair = jnp.concatenate(
                    (rows_ref[head, gap : gap + 1, :], rows_ref[head, gap + 1 : gap + 2, :]),
                    axis=1,
                )
                spread = jnp.broadcast_to(pair, (size, 2 * size))
                spread = pltpu.roll(spread, 0, 1, stride=1, stride_axis=0)
                tiles_ref[head, part, step + 1] = spread[:, :size]
        return carry

    lax.fori_loop(0, heads, head_step, 0)


def cost(us):
    return pl.CostEstimate(flops=0, bytes_accessed=int(us * 3.4e6), transcendentals=0)


def bias_tiles(rows, inner):
    heads, count, size = rows.shape
    return pl.pallas_call(
        bias_kernel,
        out_shape=jax.ShapeDtypeStruct((heads, inner, (count - 1) // inner + 1, size, size), F32),
        cost_estimate=cost(0.05),
        name="bias_tiles",
    )(rows)


def block_of(kv_refs, slot, kb):
    if len(kv_refs) == 1:
        return kv_refs[0][slot, kb]
    return kv_refs[slot][kb]


def bias_place(place_ref, slot):
    shift = place_ref[0] - place_ref[2 + slot]
    below = (shift < 0).astype(jnp.int32)
    return shift + below * place_ref[1], 1 - below


def forward_kernel(
    place_ref,
    q_ref,
    *refs,
):
    groups, size, _ = q_ref.shape
    kv_refs, (start_ref, bias_ref, out_ref, full_ref, lse_ref, s_ref, vs_ref) = refs[:-7], refs[-7:]
    slots = s_ref.shape[0]
    tall = GHEADS * size

    def spread_step(slot, carry):
        for kb in range(groups):
            vs_ref[slot, kb] = heads_apart(block_of(kv_refs, slot, kb)[:, GW:], 1)
        return carry

    loop(slots, spread_step, 0)
    for qb in range(groups):
        queries = heads_apart(q_ref[qb], 0.125)
        start = start_ref[qb]
        query_block = qb * place_ref[1] + place_ref[0]

        def score_step(slot, top):
            part, tile = bias_place(place_ref, slot)
            for kb in range(qb + 1):
                key_block = kb * place_ref[1] + place_ref[2 + slot]
                mask = tile_mask(start, query_block, key_block, size)
                raw = dotf(queries, block_of(kv_refs, slot, kb)[:, :GW], NT)
                bias = [bias_ref[head, part, tile + qb - kb] + mask for head in range(GHEADS)]
                score = raw + jnp.concatenate(bias, axis=0)
                s_ref[slot, kb] = score
                top = jnp.maximum(top, score)
            return top

        top = loop(slots, score_step, jnp.full((tall, size), -1e30, F32))
        top = jnp.broadcast_to(jnp.max(top, axis=1, keepdims=True), (tall, size))

        def exp_step(slot, total):
            for kb in range(qb + 1):
                value = jnp.exp(s_ref[slot, kb] - top)
                s_ref[slot, kb] = value
                total = total + value
            return total

        total = loop(slots, exp_step, jnp.zeros((tall, size), F32))
        total = jnp.broadcast_to(jnp.sum(total, axis=1, keepdims=True), (tall, size))
        scale = 1.0 / total
        lse_ref[qb] = top + jnp.log(total)

        def out_step(slot, sums):
            low_sum, rest_sum = sums
            for kb in range(qb + 1):
                prob = s_ref[slot, kb] * scale
                prob_low = prob.astype(BF)
                rest = (prob - prob_low.astype(F32)).astype(BF)
                values = vs_ref[slot, kb]
                low_sum = low_sum + dotf(heads_beside(prob_low, size), values)
                rest_sum = rest_sum + dotf(heads_beside(rest, size), values)
            return (low_sum, rest_sum)

        zero = jnp.zeros((size, GW), F32)
        low_sum, rest_sum = loop(slots, out_step, (zero, zero))
        full_ref[qb] = low_sum + rest_sum
        out_ref[qb] = turned(low_sum).astype(BF)


VM = pl.BlockSpec(memory_space=pltpu.VMEM)
SM = pl.BlockSpec(memory_space=pltpu.SMEM)


def attention_forward(place, q, kv, start, bias):
    groups, size, _ = q.shape
    slots = kv[0].shape[0] if len(kv) == 1 else len(kv)
    return pl.pallas_call(
        forward_kernel,
        in_specs=[SM] + [VM] * (3 + len(kv)),
        out_specs=[VM] * 3,
        out_shape=(
            jax.ShapeDtypeStruct((groups, GW, size), BF),
            jax.ShapeDtypeStruct((groups, size, GW), F32),
            jax.ShapeDtypeStruct((groups, GHEADS * size, size), F32),
        ),
        scratch_shapes=[
            pltpu.VMEM((slots, groups, GHEADS * size, size), F32),
            pltpu.VMEM((slots, groups, GHEADS * size, GW), BF),
        ],
        cost_estimate=cost(7),
        name="attention_forward",
    )(place, q, *kv, start, bias)


def backward_kernel(
    place_ref,
    q_ref,
    kv_ref,
    start_ref,
    bias_ref,
    lse_ref,
    full_ref,
    out_grad_ref,
    dq_ref,
    dkv_ref,
    dist_ref,
    dist_acc,
    qs_ref,
    gs_ref,
    delta_ref,
    dkv_acc,
):
    groups, size, _ = q_ref.shape
    slots = kv_ref.shape[0]
    tall = GHEADS * size
    for block in range(groups):
        spread = heads_apart(turned_back(out_grad_ref[block].astype(F32)).astype(BF), 1)
        gs_ref[block] = spread
        full = full_ref[block]
        product = spread.astype(F32) * jnp.concatenate([full] * GHEADS, axis=0)
        delta = jnp.sum(product, axis=1, keepdims=True)
        delta_ref[block] = jnp.broadcast_to(delta, (tall, size))
    for qb in range(groups):
        qs_ref[qb] = heads_apart(q_ref[qb], 0.125)
    dq_ref[...] = jnp.zeros_like(dq_ref)

    def slot_step(slot, carry):
        dist_acc[...] = jnp.zeros_like(dist_acc)
        part, tile = bias_place(place_ref, slot)
        dkv_acc[...] = jnp.zeros_like(dkv_acc)

        def pair(kb, qb):
            key_block = kb * place_ref[1] + place_ref[2 + slot]
            query_block = qb * place_ref[1] + place_ref[0]
            key, value = kv_ref[slot, kb, :, :GW], kv_ref[slot, kb, :, GW:]
            mask = tile_mask(start_ref[qb], query_block, key_block, size)
            at = tile + qb - kb
            bias = [bias_ref[head, part, at] + mask for head in range(GHEADS)]
            queries, grads = qs_ref[qb], gs_ref[qb]
            raw = dotf(queries, key, NT)
            prob_grad = dotf(grads, value, NT)
            prob = jnp.exp(raw + (jnp.concatenate(bias, axis=0) - lse_ref[qb]))
            score_grad = (prob * (prob_grad - delta_ref[qb])).astype(BF)
            dk = dotf(score_grad, queries, TN)
            dv = dotf(prob.astype(BF), grads, TN)
            dq = dotf(heads_beside(score_grad, size), heads_apart(key, 0.125))
            return kb, qb, at, score_grad, dk, dv, dq

        def add(kb, qb, at, score_grad, dk, dv, dq):
            for head in range(GHEADS):
                dist_acc[head, at] += score_grad[head * size : (head + 1) * size].astype(F32)
            dkv_acc[kb, :, :GW] += dk
            dkv_acc[kb, :, GW:] += dv
            dq_ref[qb] += dq

        def pair_step(step, carry):
            last = (step == groups).astype(jnp.int32)
            late = (step >= groups - 1).astype(jnp.int32)
            one = pair(3 * last, step - last)
            two = pair(1 + late, step + 1 - 2 * late)
            add(*one)
            add(*two)
            return carry

        lax.fori_loop(0, groups + 1, pair_step, 0)
        dkv_ref[slot] = dkv_acc[...].astype(dkv_ref.dtype)
        row = lax.broadcasted_iota(jnp.int32, (size, size), 0)
        lane = lax.broadcasted_iota(jnp.int32, (size, size), 1)
        flip = (row + lane == size - 1).astype(F32)
        for head in range(GHEADS):
            tiles = jnp.concatenate(
                [dist_acc[head, step] for step in range(groups + 1)], axis=1
            )
            tiles = jnp.dot(flip, tiles, precision=HIGHEST)
            for step in range(groups + 1):
                tile_rows = tiles[:, step * size : (step + 1) * size]
                wide = jnp.concatenate((tile_rows, jnp.zeros_like(tile_rows)), axis=1)
                wide = pltpu.roll(wide, 1, 1, stride=1, stride_axis=0)
                dist_ref[slot, head, step : step + 1, :] = jnp.sum(wide, axis=0, keepdims=True)
        return carry

    loop(slots, slot_step, 0)


def attention_backward(place, q, kv, start, bias, lse, full, out_grad, dtype, us):
    groups, size, _ = q.shape
    slots = kv.shape[0]
    tall = GHEADS * size
    return pl.pallas_call(
        backward_kernel,
        in_specs=[SM] + [VM] * 7,
        out_specs=[VM] * 3,
        out_shape=(
            jax.ShapeDtypeStruct((groups, size, GW), F32),
            jax.ShapeDtypeStruct((slots, groups, size, 2 * GW), dtype),
            jax.ShapeDtypeStruct((slots, GHEADS, groups + 1, 2 * size), F32),
        ),
        scratch_shapes=[
            pltpu.VMEM((GHEADS, groups + 1, size, size), F32),
            pltpu.VMEM((groups, tall, GW), BF),
            pltpu.VMEM((groups, tall, GW), BF),
            pltpu.VMEM((groups, tall, size), F32),
            pltpu.VMEM((groups, size, 2 * GW), F32),
        ],
        cost_estimate=cost(us),
        name="attention_backward",
    )(place, q, kv, start, bias, lse, full, out_grad)


def project_kernel(own_ref, h0_ref, h1_ref, h2_ref, h3_ref, w_ref, q_ref, kv_ref, h_ref):
    groups, size, _ = h_ref.shape
    for step, piece_ref in enumerate((h0_ref, h1_ref, h2_ref, h3_ref)):
        h_ref[behind(step, own_ref[0], groups)] = piece_ref[...]
    rows = dotf(h_ref[...].reshape(groups * size, D), w_ref[...]).astype(BF)
    q_ref[...] = rows[:, :GW].reshape(groups, size, GW)
    kv_ref[...] = rows[:, GW:].reshape(groups, size, 2 * GW)


def project(own, pieces, w_cols):
    size = pieces[0].shape[0]
    return pl.pallas_call(
        project_kernel,
        in_specs=[SM] + [VM] * 5,
        out_specs=[VM] * 3,
        out_shape=(
            jax.ShapeDtypeStruct((GROUPS, size, GW), BF),
            jax.ShapeDtypeStruct((GROUPS, size, 2 * GW), BF),
            jax.ShapeDtypeStruct((GROUPS, size, D), BF),
        ),
        cost_estimate=cost(0.05),
        name="project",
    )(own, *pieces, w_cols)


def mlp_in_kernel(
    att_ref, w_ref, x_ref, gain_ref, disp_ref, resid_ref, sent_ref
):
    total = x_ref[...]
    for group in range(GROUPS):
        total = total + dotf(att_ref[group], w_ref[group], TN)
    resid_ref[...] = total
    rate = lax.rsqrt(jnp.mean(total * total, axis=-1, keepdims=True) + EPS)
    low = (total * rate * gain_ref[...]).astype(BF)
    sent_ref[...] = dotf(disp_ref[...], low).astype(BF)


def mlp_in(att, w_attn, x, gain, disp):
    return pl.pallas_call(
        mlp_in_kernel,
        in_specs=[VM] * 5,
        out_specs=[VM] * 2,
        out_shape=(
            jax.ShapeDtypeStruct(x.shape, F32),
            jax.ShapeDtypeStruct((disp.shape[0], D), BF),
        ),
        cost_estimate=cost(0.05),
        name="mlp_in",
    )(att, w_attn, x, gain, disp)


def expert_kernel(
    own_ref,
    x_ref,
    came_ref,
    w_in_ref,
    w_out_ref,
    router_ref,
    active_ref,
    hidden_grad_ref,
    out_grad_ref,
    back_ref,
    out_ref,
    router_grad_ref,
    out_acc,
    back_acc,
    gate_ref,
):
    step = pl.program_id(0)
    rows = x_ref[...]
    lane = lax.broadcasted_iota(jnp.int32, (rows.shape[0], 128), 1)

    @pl.when(step == 0)
    def _():
        logits = dotf(rows, router_ref[...])
        pair = came_ref[:, D:].astype(F32)
        own = jnp.sum(jnp.where(lane == own_ref[0], logits, 0.0), axis=1, keepdims=True)
        other = jnp.where(lane == own_ref[0], 0.0, pair)
        other = jnp.sum(other * logits, axis=1, keepdims=True)
        peak = jnp.maximum(own, other)
        own_e, other_e = jnp.exp(own - peak), jnp.exp(other - peak)
        total = own_e + other_e
        own_gate = own_e / total
        gate_ref[0] = jnp.broadcast_to(own_gate, lane.shape)
        gate_ref[1] = jnp.broadcast_to(other_e / total, lane.shape)
        out_grad_ref[...] = (own_gate * came_ref[:, :D].astype(F32)).astype(BF)
        out_acc[...] = jnp.zeros_like(out_acc)
        back_acc[...] = jnp.zeros_like(back_acc)

    half = rows.shape[0] // 2

    def half_step(part, carry):
        at = pl.ds(pl.multiple_of(part * half, half), half)
        hidden = dotf(x_ref[at, :], w_in_ref[...])
        active_grad = dotf(out_grad_ref[at, :], w_out_ref[...], NT)
        value, slope = gelu_parts(hidden)
        active = value.astype(BF)
        hidden_grad = (slope * active_grad).astype(BF)
        active_ref[at, :] = active
        hidden_grad_ref[at, :] = hidden_grad
        out_acc[at, :] += dotf(active, w_out_ref[...])
        back_acc[at, :] += dotf(hidden_grad, w_in_ref[...], NT)
        return carry

    lax.fori_loop(0, 2, half_step, 0)

    @pl.when(step == pl.num_programs(0) - 1)
    def _():
        produced = out_acc[...].astype(BF).astype(F32)
        own_gate, other_gate = gate_ref[0][:, :1], gate_ref[1][:, :1]
        out_ref[...] = (own_gate * produced).astype(BF)
        gate_grad = jnp.sum(came_ref[:, :D].astype(F32) * produced, axis=1, keepdims=True)
        pull = own_gate * other_gate * gate_grad
        pair = came_ref[:, D:].astype(F32)
        logit_rows = pull * jnp.where(lane == own_ref[0], 1.0, -pair)
        high = logit_rows.astype(BF)
        rest = (logit_rows - high.astype(F32)).astype(BF)
        router = router_ref[...]
        back = back_acc[...].astype(BF).astype(F32)
        back = back + dotf(high, router, NT) + dotf(rest, router, NT)
        back_ref[...] = back.astype(BF)
        router_grad_ref[...] = dotf(rows, high, TN) + dotf(rows, rest, TN)


def expert_layer(own, x, came, w_in, w_out, router):
    count = x.shape[0]
    steps = 4
    part = FF // steps
    whole = lambda *shape: pl.BlockSpec(shape, lambda f, own: (0,) * len(shape))
    piece = pl.BlockSpec((count, part), lambda f, own: (0, own[1 + f]))
    return pl.pallas_call(
        expert_kernel,
        grid_spec=pltpu.PrefetchScalarGridSpec(
            num_scalar_prefetch=1,
            grid=(steps,),
            in_specs=[
                whole(count, D),
                whole(count, D + 128),
                pl.BlockSpec((D, part), lambda f, own: (0, f)),
                pl.BlockSpec((part, D), lambda f, own: (f, 0)),
                whole(D, 128),
            ],
            out_specs=[
                piece,
                piece,
                whole(count, D),
                whole(count, D),
                whole(count, D),
                whole(D, 128),
            ],
            scratch_shapes=[
                pltpu.VMEM((count, D), F32),
                pltpu.VMEM((count, D), F32),
                pltpu.VMEM((2, count, 128), F32),
            ],
        ),
        out_shape=(
            jax.ShapeDtypeStruct((count, FF), BF),
            jax.ShapeDtypeStruct((count, FF), BF),
            jax.ShapeDtypeStruct((count, D), BF),
            jax.ShapeDtypeStruct((count, D), BF),
            jax.ShapeDtypeStruct((count, D), BF),
            jax.ShapeDtypeStruct((D, 128), F32),
        ),
        cost_estimate=cost(0.05),
        name="expert_layer",
    )(own, x, came, w_in, w_out, router)


def mlp_back_kernel(
    back_ref, disp_ref, resid_ref, up_ref, gain_ref, w_ref, grad_ref, low_ref, gain_grad_ref, out_ref
):
    grad = dotf(disp_ref[...], back_ref[...], TN)
    resid = resid_ref[...]
    rate = lax.rsqrt(jnp.mean(resid * resid, axis=-1, keepdims=True) + EPS)
    unit = resid * rate
    gain_grad_ref[...] = jnp.sum(grad * unit, axis=0, keepdims=True)
    scaled = grad * gain_ref[...]
    total = up_ref[...] + rate * (
        scaled - unit * jnp.mean(scaled * unit, axis=-1, keepdims=True)
    )
    grad_ref[...] = total
    low = total.astype(BF)
    low_ref[...] = low
    for group in range(GROUPS):
        out_ref[group] = dotf(w_ref[group], low, NT).astype(BF)


def mlp_back(back, disp, resid, up, gain, w_attn):
    size = resid.shape[0]
    return pl.pallas_call(
        mlp_back_kernel,
        in_specs=[VM] * 6,
        out_specs=[VM] * 4,
        out_shape=(
            jax.ShapeDtypeStruct((size, D), F32),
            jax.ShapeDtypeStruct((size, D), BF),
            jax.ShapeDtypeStruct((1, D), F32),
            jax.ShapeDtypeStruct((GROUPS, GW, size), BF),
        ),
        cost_estimate=cost(4),
        name="mlp_back",
    )(back, disp, resid, up, gain, w_attn)


def project_back_kernel(
    dq_ref,
    dq_other_ref,
    dkv_ref,
    came_ref,
    w_ref,
    h_ref,
    gain_ref,
    dproj_ref,
    gain_grad_ref,
    half_ref,
):
    groups, size, _ = dq_ref.shape
    dq = (dq_ref[...] + dq_other_ref[...]).astype(BF).reshape(groups * size, GW)
    dkv = (dkv_ref[...] + came_ref[...].astype(F32)).astype(BF)
    dkv = dkv.reshape(groups * size, 2 * GW)
    dproj_ref[...] = jnp.concatenate((dq, dkv), axis=1)
    total = jnp.zeros((1, D), F32)
    for block in range(groups):
        half = dotf(dproj_ref[block * size : (block + 1) * size], w_ref[...], NT)
        half_ref[block] = half.astype(BF)
        total = total + jnp.sum(half * h_ref[block].astype(F32), axis=0, keepdims=True)
    gain_grad_ref[...] = total / gain_ref[...]


def project_back(dq, dq_other, dkv, came, w_cols, h_col, gain):
    groups, size, _ = dq.shape
    return pl.pallas_call(
        project_back_kernel,
        in_specs=[VM] * 7,
        out_specs=[VM] * 3,
        out_shape=(
            jax.ShapeDtypeStruct((groups * size, 3 * GW), BF),
            jax.ShapeDtypeStruct((1, D), F32),
            jax.ShapeDtypeStruct((groups, size, D), BF),
        ),
        cost_estimate=cost(4),
        name="project_back",
    )(dq, dq_other, dkv, came, w_cols, h_col, gain)


def qkv_grad_kernel(h_ref, dproj_ref, grad_ref):
    ranks, rows, _ = grad_ref.shape
    groups, size, _ = h_ref.shape
    total = dotf(h_ref[...].reshape(groups * size, D), dproj_ref[...], TN)
    for rank in range(ranks):
        grad_ref[rank] = total[rank * rows : (rank + 1) * rows]


def qkv_grad_of(h_col, dproj, ranks):
    return pl.pallas_call(
        qkv_grad_kernel,
        in_specs=[VM] * 2,
        out_specs=VM,
        out_shape=jax.ShapeDtypeStruct((ranks, D // ranks, 3 * GW), F32),
        cost_estimate=cost(0.05),
        name="qkv_grad",
    )(h_col, dproj)


def side_grad_kernel(att_ref, grad_ref, router_ref, out_ref):
    ranks, rows, _ = out_ref.shape
    inner = ranks // GROUPS
    for block in range(GROUPS):
        total = dotf(att_ref[block], grad_ref[...])
        for part in range(inner):
            out_ref[block * inner + part, :, :D] = total[part * rows : (part + 1) * rows]
    for rank in range(ranks):
        out_ref[rank, :, D:] = router_ref[rank * rows : (rank + 1) * rows]


def side_grad_of(att, grad, router_grad, ranks):
    return pl.pallas_call(
        side_grad_kernel,
        in_specs=[VM] * 3,
        out_specs=VM,
        out_shape=jax.ShapeDtypeStruct((ranks, D // ranks, D + 128), F32),
        cost_estimate=cost(0.05),
        name="side_grad",
    )(att, grad, router_grad)


def assemble_kernel(own_ref, p0_ref, p1_ref, p2_ref, p3_ref, rows_ref, scratch):
    side = D + 128
    wide = side + 3 * GW
    last = side + 3 * D
    width = (p0_ref.shape[1] - wide) // 2
    pieces = [ref[...].astype(F32) for ref in (p0_ref, p1_ref, p2_ref, p3_ref)]
    total = pieces[0] + pieces[1] + pieces[2] + pieces[3]
    rows_ref[:, :side] = total[:, :side].astype(BF)
    small = total[:, wide : wide + width] + total[:, wide + width :]
    high = small.astype(BF)
    rows_ref[:, last : last + width] = high
    rows_ref[:, last + width :] = (small - high.astype(F32)).astype(BF)
    for step, piece in enumerate(pieces):
        scratch[behind(step, own_ref[0], GROUPS)] = piece[:, side:wide]
    for group in range(GROUPS):
        for kind in range(3):
            at = side + (kind * GROUPS + group) * GW
            rows_ref[:, at : at + GW] = scratch[group, :, kind * GW : (kind + 1) * GW].astype(BF)


def assemble(own, parts):
    rows, width = parts[0].shape
    return pl.pallas_call(
        assemble_kernel,
        in_specs=[SM] + [VM] * 4,
        out_specs=VM,
        out_shape=jax.ShapeDtypeStruct((rows, width + 3 * D - 3 * GW), BF),
        scratch_shapes=[pltpu.VMEM((GROUPS, rows, 3 * GW), F32)],
        cost_estimate=cost(0.05),
        name="assemble",
    )(own, *parts)


def unpack_kernel(own_ref, pair_ref, came_ref, attn_ref, router_ref, qkv_ref, small_ref):
    experts = router_ref.shape[2]
    last = 4 * D + 128
    width = small_ref.shape[1]
    small = jnp.zeros(small_ref.shape, F32)
    for near, ref in ((own_ref[0], pair_ref), (1 - own_ref[0], came_ref)):
        for part in range(2):
            value = ref[part].astype(F32)
            attn_ref[near * 2 + part] = value[:, :D]
            router_ref[near * 2 + part] = value[:, D : D + experts]
            qkv_ref[near * 2 + part] = value[:, D + 128 : last]
            small = small + (value[:, last : last + width] + value[:, last + width :])
    small_ref[...] = small


def unpack(own, pair, came, experts):
    rows = pair.shape[1]
    width = (pair.shape[2] - 4 * D - 128) // 2
    outs = pl.pallas_call(
        unpack_kernel,
        in_specs=[SM] + [VM] * 2,
        out_specs=[VM] * 4,
        out_shape=[jax.ShapeDtypeStruct((4, rows, n), F32) for n in (D, experts, 3 * D)]
        + [jax.ShapeDtypeStruct((rows, width), F32)],
        cost_estimate=cost(0.05),
        name="unpack",
    )(own.astype(jnp.int32), pair, came)
    return [out.reshape(4 * rows, -1) for out in outs[:3]] + [outs[3]]


def gelu_parts(hidden):
    scale = math.sqrt(2.0 / math.pi)
    square = hidden * hidden
    bend = jnp.tanh(hidden * (scale + (scale * 0.044715) * square))
    half = 0.5 + 0.5 * bend
    slope = scale + (3 * scale * 0.044715) * square
    return hidden * half, half + (0.5 * hidden) * (1.0 - bend * bend) * slope


def swap(value, axis):
    return lax.ppermute(value, axis, [(0, 1), (1, 0)])


def tie(*values):
    return lax.optimization_barrier(values)


def turn(value, step):
    return lax.ppermute(value, "g", [(j, (j + step) % GROUPS) for j in range(GROUPS)])


def in_turn(pieces, g):
    pieces = jnp.stack(pieces[::-1] * 2)
    return lax.dynamic_slice_in_dim(pieces, GROUPS - 1 - g, GROUPS, 0)


def exchange(value, axes):
    return lax.all_to_all(value, axes, split_axis=0, concat_axis=0, tiled=True)


def in_order(own, came, index):
    return jnp.where(index == 0, jnp.stack((own, came)), jnp.stack((came, own)))


def rep_gather(value, y, c):
    pair = in_order(value, swap(value, "y"), y)
    return in_order(pair, swap(pair, "c"), c)


def halve(value, index, axis):
    count, rows, cols = value.shape
    value = value.reshape(count, 2, rows // 2, cols)
    away = swap(pick(value, 1 - index, 1).astype(BF), axis)
    return pick(value, index, 1) + away.astype(F32)


def pick(value, index, axis):
    return lax.dynamic_index_in_dim(value, index, axis, keepdims=False)


def norm_backward(grad, gain, value):
    rate = lax.rsqrt(jnp.mean(value * value, axis=-1, keepdims=True) + EPS)
    unit = value * rate
    scaled = grad * gain
    return rate * (scaled - unit * jnp.mean(scaled * unit, axis=-1, keepdims=True))


def local(
    tokens,
    cotangent,
    gain_attn,
    gain_mlp,
    w_qkv,
    w_attn_out,
    router,
    rel_table,
    w_in,
    w_out,
    segment_ids,
    expert_ids,
    rel_bucket,
):
    groups, inner = lax.axis_size("g"), lax.axis_size("i")
    g, i = lax.axis_index("g"), lax.axis_index("i")
    y, c = lax.axis_index("y"), lax.axis_index("c")
    ranks = groups * inner
    copies = 4
    size = tokens.shape[1]
    experts = ranks
    capacity = max(2, 4 * size // experts)
    inputs = tokens[0]
    upstream = cotangent[0]
    seg_all = segment_ids[0]
    chosen_ids = expert_ids[0]
    rows = w_qkv.shape[0] // copies
    me = g * inner + i
    own_g = g[None].astype(jnp.int32)

    rate = lax.rsqrt(jnp.mean(inputs * inputs, axis=-1, keepdims=True) + EPS)
    h_attn = (inputs * rate * gain_attn).astype(BF)
    h_pieces = [h_attn] + [turn(h_attn, step) for step in range(1, groups)]

    part = lax.dynamic_slice_in_dim(w_qkv, c * 2 * rows, 2 * rows, 0).astype(BF)
    part = part.reshape(2 * rows, 3, groups, GW).transpose(2, 0, 1, 3)
    part = jnp.broadcast_to(part[:, None], (groups, inner, 2 * rows, 3, GW))
    part = exchange(part.reshape(ranks, 2 * rows, 3 * GW), SEQ)
    both = jnp.concatenate((w_attn_out, jnp.pad(router, ((0, 0), (0, 128 - experts)))), axis=1)
    both = lax.dynamic_slice_in_dim(both, (c * 2 + y) * rows, rows, 0).astype(BF)
    both = jnp.broadcast_to(both[None], (ranks, rows, D + 128))
    w_cols = in_order(part, swap(part, "c"), c).swapaxes(0, 1).reshape(D, 3 * GW)

    expert_iota = jnp.arange(experts, dtype=jnp.int32)
    token_iota = jnp.arange(size, dtype=jnp.int32)
    pair_hot = jnp.any(chosen_ids[:, :, None] == expert_iota[None, None, :], axis=1)
    rank = jnp.dot(
        (token_iota[:, None] > token_iota[None, :]).astype(BF),
        pair_hot.astype(BF),
        preferred_element_type=F32,
    ).astype(jnp.int32)
    disp = (rank.T[:, None, :] == jnp.arange(capacity, dtype=jnp.int32)[None, :, None]) & (
        pair_hot.T[:, None, :]
    )
    disp = disp.astype(BF).reshape(experts * capacity, size)
    early = jnp.concatenate(
        (upstream.astype(BF), jnp.pad(pair_hot.astype(BF), ((0, 0), (0, 128 - experts)))), axis=1
    )
    early = jnp.dot(disp, early, preferred_element_type=F32).astype(BF)
    seg_col = pick(seg_all.reshape(groups, inner, size), i, 1)
    start = jnp.sum(
        (seg_all[None, None, :] < seg_col[:, :, None]).astype(jnp.int32), axis=-1, keepdims=True
    )
    padded = jnp.concatenate(
        (jnp.full((size - 1,), -1, jnp.int32), rel_bucket, jnp.full((1,), -1, jnp.int32))
    )
    reversed_bucket = padded.reshape(ranks + 1, size)[:, ::-1].reshape(-1)
    bucket_hot = (
        jnp.arange(BUCKETS, dtype=jnp.int32)[:, None] == reversed_bucket[None, :]
    ).astype(F32)
    table = lax.dynamic_slice_in_dim(rel_table, g * GHEADS, GHEADS, 0)
    bias_rows = jnp.dot(table, bucket_hot, precision=HIGHEST).reshape(GHEADS, ranks + 1, size)
    bias = bias_tiles(bias_rows, inner)
    bias, start, *h_pieces = tie(bias, start, *h_pieces)

    early = jnp.concatenate((early.reshape(ranks, capacity, D + 128), both), axis=1)
    early, *h_pieces = tie(early, *h_pieces)
    q, kv, h_col = project(own_g, h_pieces, w_cols)
    came_rows = exchange(early, SEQ)
    head_place = jnp.stack((i, jnp.int32(inner)))

    def place_of(columns):
        return jnp.concatenate((head_place, columns, own_g)).astype(jnp.int32)

    if inner == 2:
        kv_came = swap(kv, "i")
        kv_all = (kv, kv_came)
        columns = jnp.stack((i, 1 - i))
    else:
        kv_all = (lax.all_gather(kv, "i"),)
        columns = jnp.arange(inner, dtype=jnp.int32)
    place = place_of(columns)
    mixed, mixed_full, lse = attention_forward(place, q, kv_all, start, bias)
    mixed, came_rows = tie(mixed, came_rows)
    both = came_rows[:, capacity:]
    both = in_order(both, swap(both, "y"), y)
    came_rows = came_rows[:, :capacity].reshape(ranks * capacity, D + 128)
    att = exchange(mixed, "g")
    att, both = tie(att, both)
    both = in_order(both, swap(both, "c"), c)
    both = both.transpose(2, 0, 1, 3, 4).reshape(D, D + 128)
    w_attn_low = both[:, :D].reshape(groups, GW, D)
    router_low = both[:, D:]
    residual, outgoing = mlp_in(att, w_attn_low, inputs, gain_mlp[None], disp)

    arrived = exchange(outgoing.reshape(ranks, capacity, D), SEQ).reshape(ranks * capacity, D)
    active, hidden_grad, produced_grad, back, produced, router_grad = expert_layer(
        jnp.stack([me] + [2 * (c == f % 2) + (y == f // 2) for f in range(4)]).astype(jnp.int32),
        arrived,
        came_rows, w_in[0], w_out[0], router_low
    )
    back_rows = exchange(back.reshape(ranks, capacity, D), SEQ).reshape(ranks * capacity, D)

    part_ff = FF // 4
    slices = [slice(f * part_ff, (f + 1) * part_ff) for f in range(4)]

    def part_grads(f, active=active, hidden_grad=hidden_grad):
        return (
            dotf(active[:, slices[f]], produced_grad, TN),
            dotf(arrived, hidden_grad[:, slices[f]], TN),
        )

    core_far = [swap(grad.astype(BF), "c") for grad in part_grads(0)]
    near = [grad.astype(BF) for grad in part_grads(1)]
    away = [
        (grad + core.astype(F32)).astype(BF) for grad, core in zip(part_grads(2), core_far)
    ]
    far_out = swap(away[0], "y")
    back_rows, *near = tie(back_rows, *near)

    resid_grad, attn_grad, gain_two, out_grad = mlp_back(
        back_rows, disp, residual, upstream, gain_mlp[None], w_attn_low
    )
    out_grad = exchange(out_grad, "g")
    side_grad = side_grad_of(att, attn_grad, router_grad, ranks)
    out_grad, produced, side_grad, away_in = tie(out_grad, produced, side_grad, away[1])
    far_in = swap(away_in, "y")
    near = [swap(grad, "c") for grad in near]
    returned = exchange(produced.reshape(ranks, capacity, D), SEQ)

    def inner_reduce(value):
        value = value.reshape(groups, inner, *value.shape[1:])
        if inner > 2:
            return lax.psum_scatter(value, "i", scatter_dimension=1).astype(BF)
        own = pick(value, i, 1) + swap(pick(value, 1 - i, 1).astype(BF), "i").astype(F32)
        return own.astype(BF)

    if inner == 2:
        dq_other, dkv_other, dist_other = attention_backward(
            place_of(1 - i[None]),
            q,
            kv_came[None],
            start,
            bias,
            lse,
            mixed_full,
            out_grad,
            BF,
            8,
        )
        out_grad, dq_other, dkv_other, far_out = tie(out_grad, dq_other, dkv_other, far_out)
        dkv_came = swap(dkv_other[0], "i")
        dq, dkv_own, dist = attention_backward(
            place_of(i[None]),
            q,
            kv[None],
            start,
            bias,
            lse,
            mixed_full,
            out_grad,
            F32,
            1,
        )
        dkv_own = dkv_own[0]
        dist = jnp.concatenate((dist, dist_other))
    else:
        dq, dkv_all, dist = attention_backward(
            place, q, kv_all[0], start, bias, lse, mixed_full, out_grad, F32, 1
        )
        dkv_own = lax.psum_scatter(dkv_all, "i")
        dkv_came = jnp.zeros(dkv_own.shape, BF)
        dq_other = jnp.zeros_like(dq)
        dist = jnp.take(dist, (i - jnp.arange(inner)) % inner, axis=0)
    dkv_own, returned, far_in = tie(dkv_own, returned, far_in)
    returned = returned.reshape(ranks * capacity, D)
    dproj, gain_one, half = project_back(
        dq, dq_other, dkv_own, dkv_came, w_cols, h_col, gain_attn[None]
    )
    half = exchange(half, "g")
    dproj, side_grad = tie(dproj, side_grad)
    side_grad = halve(side_grad, c, "c")
    dproj, side_grad = tie(dproj, side_grad)
    parts = halve(qkv_grad_of(h_col, dproj, ranks), c, "c")
    parts, gain_one, gain_two, dist = tie(
        jnp.concatenate((side_grad, parts), axis=2), gain_one, gain_two, dist
    )
    parts = halve(parts, y, "y")
    parts, half, active, hidden_grad, *near = tie(parts, half, active, hidden_grad, *near)
    mine_out, mine_in = [
        grad + core.astype(F32) for grad, core in zip(part_grads(3, active, hidden_grad), near)
    ]
    dist = dist[:, :, 1:].transpose(1, 2, 0, 3).reshape(GHEADS, ranks, 2 * size)
    dist_rows = jnp.pad(dist[:, :, size:], ((0, 0), (0, 1), (0, 0))) + jnp.pad(
        dist[:, :, :size], ((0, 0), (1, 0), (0, 0))
    )
    table_grad = jnp.dot(dist_rows.reshape(GHEADS, -1), bucket_hot.T, precision=HIGHEST)
    table_all = lax.dynamic_update_slice(
        jnp.zeros((HEADS, BUCKETS), F32), table_grad, (g * GHEADS, 0)
    )
    small = jnp.concatenate((gain_one[0], gain_two[0], table_all.reshape(-1)))
    count = small.shape[0]
    width = -(-count // (rows * 128)) * 128
    small = jnp.pad(small.reshape(-1, 128), ((0, (rows * width - count) // 128), (0, 0)))
    small = small.reshape(rows, width)
    small = small + (swap(small, "i") if inner == 2 else lax.psum(small, "i") - small)
    high = lax.reduce_precision(small, 8, 7)
    small = jnp.concatenate((high, small - high), axis=1).astype(BF)
    small = jnp.broadcast_to(small[None], (groups, rows, 2 * width))

    parts = jnp.concatenate((inner_reduce(parts), small), axis=2)
    parts = [pick(parts, g, 0)] + [
        turn(pick(parts, lax.rem(g + step, groups), 0), step) for step in range(1, groups)
    ]
    norm_in_grad = jnp.sum(half.astype(F32), axis=0)
    input_grad = resid_grad + norm_backward(norm_in_grad, gain_attn, inputs)
    result = residual + dotf(disp, returned, TN)
    shards = assemble(own_g, parts)
    pair = in_order(shards, swap(shards, "y"), y)
    attn_shard, router_shard, qkv_shard, small = unpack(c[None], pair, swap(pair, "c"), experts)
    small = small.reshape(-1)
    w_in_shard = mine_in + far_in.astype(F32)
    w_out_shard = mine_out + far_out.astype(F32)
    return (
        result[None],
        input_grad[None],
        small[:D],
        small[D : 2 * D],
        qkv_shard,
        attn_shard,
        router_shard,
        small[2 * D : 2 * D + HEADS * BUCKETS].reshape(HEADS, BUCKETS),
        w_in_shard[None],
        w_out_shard[None],
    )


def solution(mesh):
    ranks = mesh.shape["seq"]
    split = Mesh(
        mesh.devices.reshape(2, mesh.shape["rep"] // 2, GROUPS, ranks // GROUPS),
        ("y", "c", "g", "i"),
    )
    placed = (
        P(REP, SEQ, None),
        P(REP, SEQ, None),
        P(),
        P(),
        P(SEQ, None),
        P(SEQ, None),
        P(SEQ, None),
        P(),
        P(SEQ, None, None),
        P(SEQ, None, None),
        P(REP, None),
        P(REP, SEQ, None),
        P(),
    )
    return jax.shard_map(
        local,
        mesh=split,
        in_specs=placed,
        out_specs=(
            P(REP, SEQ, None),
            P(REP, SEQ, None),
            P(),
            P(),
            P(SEQ, None),
            P(SEQ, None),
            P(SEQ, None),
            P(),
            P(SEQ, None, REP),
            P(SEQ, REP, None),
        ),
        check_vma=False,
    )
```

profile of v0, /device:TPU:0, one launch (start us, length us, event | category | flops | bytes accessed | tf_op | source)
XLA Modules:
  0.0 294.6 jit_solution(14224187210724693475)
XLA Ops:
  3.0 3.1 %collective-permute-start = (bf16[128,768]{1,0:T(8,128)(2,1)S(1)}, bf16[128,768]{1,0:T(8,128)(2,1)S(1)}, u32[]{:S(2)}, u32[]{:S(2)}) collective-permute-start(bf16[128,768]{1,0:T(8,128)(2,1)S(1)} %multiply_convert_fusion.h0_ref), channel_id=1, source_target_pairs={{0,2},{2,4},{4,6},{6,0},{1,3},{3,5},{5,7},{7,1},{8,10},{10,12},{12... | collective-permute-start | bytes 589832 | tf_op jit(solution)/shard_map/ppermute | solution.py:702
  12.2 3.5 %all-to-all-start = ((bf16[8,48,576]{2,1,0:T(8,128)(2,1)}), bf16[8,48,576]{2,1,0:T(8,128)(2,1)S(1)}, u32[]{:S(2)}, u32[]{:S(2)}) async-start(bf16[8,48,576]{2,1,0:T(8,128)(2,1)} %reshape.156), calls=%async_computation | async-start | bytes 983040 | tf_op jit(solution)/shard_map/all_to_all | solution.py:711
  23.8 12.5 %all-to-all-done = bf16[8,48,576]{2,1,0:T(8,128)(2,1)S(1)} async-done(((bf16[8,48,576]{2,1,0:T(8,128)(2,1)}), bf16[8,48,576]{2,1,0:T(8,128)(2,1)S(1)}, u32[]{:S(2)}, u32[]{:S(2)}) %all-to-all-start) | async-done | bytes 442400 | tf_op jit(solution)/shard_map/all_to_all | solution.py:711
  36.3 3.8 %all-to-all-start.1 = ((bf16[8,88,896]{2,1,0:T(8,128)(2,1)}), bf16[8,88,896]{2,1,0:T(8,128)(2,1)S(1)}, u32[]{:S(2)}, u32[]{:S(2)}) async-start(bf16[8,88,896]{2,1,0:T(8,128)(2,1)} %pad_maximum_fusion.1), calls=%async_computation.1 | async-start | bytes 2523136 | tf_op jit(solution)/shard_map/all_to_all | solution.py:711
  43.3 3.5 %project.1 = (bf16[4,128,192]{2,1,0:T(8,128)(2,1)}, bf16[4,128,384]{2,1,0:T(8,128)(2,1)}, bf16[4,128,768]{2,1,0:T(8,128)(2,1)}) custom-call(s32[1]{0:T(128)} %bitcast.2.own_ref, bf16[128,768]{1,0:T(8,128)(2,1)} %copy-done.18, bf16[128,768]{1,0:T(8,128)(2,1)} %copy-done.24, bf16[128,768]{1,0:T(8,128)(2,1)} %copy-done.25, bf16[128,768]{1,0:T(8,128)(2,1)} %copy-done.26, ...), custom_call_target="tpu_custom_call" | custom-call | bytes 170000 | tf_op jit(solution)/shard_map/project/pallas_call | solution.py:345
  50.2 15.2 %collective-permute-done.4.refs_1_ = bf16[4,128,384]{2,1,0:T(8,128)(2,1)S(1)} collective-permute-done((bf16[4,128,384]{2,1,0:T(8,128)(2,1)}, bf16[4,128,384]{2,1,0:T(8,128)(2,1)S(1)}, u32[]{:S(2)}, u32[]{:S(2)}) %collective-permute-start.4) | collective-permute-done | bytes 393248 | tf_op jit(solution)/shard_map/ppermute | solution.py:694
  66.1 7.2 %attention_forward.1 = (bf16[4,192,128]{2,1,0:T(8,128)(2,1)}, f32[4,128,192]{2,1,0:T(8,128)}, f32[4,384,128]{2,1,0:T(8,128)}) custom-call(s32[5]{0:T(128)} %concatenate.44.place_ref, bf16[4,128,192]{2,1,0:T(8,128)(2,1)} %get-tuple-element.92.q_ref, bf16[4,128,384]{2,1,0:T(8,128)(2,1)} %get-tuple-element.93.refs_0_, bf16[4,128,384]{2,1,0:T(8,128)(2,1)} %copy-done.14, ...), custom_call_target="tpu_custom_call" | custom-call | bytes 23800000 | tf_op jit(solution)/shard_map/attention_forward/pallas_call | solution.py:201
  75.0 6.3 %all-to-all-start.2 = ((bf16[4,192,128]{2,1,0:T(8,128)(2,1)}), bf16[4,192,128]{2,1,0:T(8,128)(2,1)S(1)}, u32[]{:S(2)}, u32[]{:S(2)}) async-start(bf16[4,192,128]{2,1,0:T(8,128)(2,1)} %get-tuple-element.98), calls=%async_computation.2 | async-start | bytes 393216 | tf_op jit(solution)/shard_map/all_to_all | solution.py:711
  83.6 5.0 %all-to-all-done.2.att_ref = bf16[4,192,128]{2,1,0:T(8,128)(2,1)S(1)} async-done(((bf16[4,192,128]{2,1,0:T(8,128)(2,1)}), bf16[4,192,128]{2,1,0:T(8,128)(2,1)S(1)}, u32[]{:S(2)}, u32[]{:S(2)}) %all-to-all-start.2) | async-done | bytes 196640 | tf_op jit(solution)/shard_map/all_to_all | solution.py:711
  92.0 3.3 %mlp_in.1 = (f32[128,768]{1,0:T(8,128)}, bf16[512,768]{1,0:T(8,128)(2,1)}) custom-call(bf16[4,192,128]{2,1,0:T(8,128)(2,1)} %copy-done.11, bf16[4,192,768]{2,1,0:T(8,128)(2,1)} %bitcast.143, f32[128,768]{1,0:T(8,128)} %bitcast.145, f32[1,768]{1,0:T(1,128)} %broadcast_in_dim.37.gain_ref, bf16[512,128]{1,0:T(8,128)(2,1)} %get-tuple-element.210.disp_ref), custom_call_target="tpu_custom_call" | custom-call | bytes 170000 | tf_op jit(solution)/shard_map/mlp_in/pallas_call | solution.py:372
  95.3 3.7 %all-to-all-start.3 = ((bf16[8,64,768]{2,1,0:T(8,128)(2,1)}), bf16[8,64,768]{2,1,0:T(8,128)(2,1)S(1)}, u32[]{:S(2)}, u32[]{:S(2)}) async-start(bf16[8,64,768]{2,1,0:T(8,128)(2,1)} %bitcast.174), calls=%async_computation.3 | async-start | bytes 1572864 | tf_op jit(solution)/shard_map/all_to_all | solution.py:711
  101.5 18.1 %all-to-all-done.3 = bf16[8,64,768]{2,1,0:T(8,128)(2,1)S(1)} async-done(((bf16[8,64,768]{2,1,0:T(8,128)(2,1)}), bf16[8,64,768]{2,1,0:T(8,128)(2,1)S(1)}, u32[]{:S(2)}, u32[]{:S(2)}) %all-to-all-start.3) | async-done | bytes 786464 | tf_op jit(solution)/shard_map/all_to_all | solution.py:711
  120.4 19.0 %expert_layer.1 = (bf16[512,3072]{1,0:T(8,128)(2,1)}, bf16[512,3072]{1,0:T(8,128)(2,1)}, bf16[512,768]{1,0:T(8,128)(2,1)}, bf16[512,768]{1,0:T(8,128)(2,1)}, bf1...) custom-call(s32[5]{0:T(128)} %stack.101.own_ref, bf16[512,768]{1,0:T(8,128)(2,1)} %bitcast.152, bf16[512,896]{1,0:T(8,128)(2,1)} %bitcast.163, ...), custom_call_target="tpu_custom_call" | custom-call | bytes 170000 | tf_op jit(solution)/shard_map/expert_layer/pallas_call | solution.py:464
  139.4 3.3 %convolution_convert_fusion = bf16[768,768]{1,0:T(8,128)(2,1)} fusion(bf16[512,768]{1,0:T(8,128)(2,1)} %get-tuple-element.108, bf16[512,3072]{1,0:T(8,128)(2,1)} %get-tuple-element.155), kind=kOutput, calls=%fused_computation.7 | convolution fusion | flops 604569600 | bytes 2752512 | tf_op jit(solution)/shard_map/dot_general | solution.py:30
  142.7 3.7 %all-to-all-start.4 = ((bf16[8,64,768]{2,1,0:T(8,128)(2,1)}), bf16[8,64,768]{2,1,0:T(8,128)(2,1)S(1)}, u32[]{:S(2)}, u32[]{:S(2)}) async-start(bf16[8,64,768]{2,1,0:T(8,128)(2,1)} %bitcast.40), calls=%async_computation.4 | async-start | bytes 1572864 | tf_op jit(solution)/shard_map/all_to_all | solution.py:711
  146.4 3.1 %convolution_convert_fusion.1 = bf16[768,768]{1,0:T(8,128)(2,1)} fusion(bf16[512,768]{1,0:T(8,128)(2,1)S(1)} %bitcast.153, bf16[512,3072]{1,0:T(8,128)(2,1)} %get-tuple-element.152), kind=kOutput, calls=%fused_computation.8 | convolution fusion | flops 604569600 | bytes 2752512 | tf_op jit(solution)/shard_map/dot_general | solution.py:30
  157.2 10.1 %all-to-all-done.4 = bf16[8,64,768]{2,1,0:T(8,128)(2,1)S(1)} async-done(((bf16[8,64,768]{2,1,0:T(8,128)(2,1)}), bf16[8,64,768]{2,1,0:T(8,128)(2,1)S(1)}, u32[]{:S(2)}, u32[]{:S(2)}) %all-to-all-start.4) | async-done | bytes 786464 | tf_op jit(solution)/shard_map/all_to_all | solution.py:711
  168.2 3.4 %mlp_back.1 = (f32[128,768]{1,0:T(8,128)}, bf16[128,768]{1,0:T(8,128)(2,1)}, f32[1,768]{1,0:T(1,128)}, bf16[4,192,128]{2,1,0:T(8,128)(2,1)}) custom-call(bf16[512,768]{1,0:T(8,128)(2,1)} %bitcast.167, bf16[512,128]{1,0:T(8,128)(2,1)} %get-tuple-element.210.disp_ref, f32[128,768]{1,0:T(8,128)} %get-tuple-element.102.resid_ref, f32[128,768]{1,0:T(8,128)} %bitcast.170, ...), custom_call_target="tpu_custom_call" | custom-call | bytes 13600000 | tf_op jit(solution)/shard_map/mlp_back/pallas_call | solution.py:524
  171.6 3.4 %all-to-all-start.5 = ((bf16[4,192,128]{2,1,0:T(8,128)(2,1)}), bf16[4,192,128]{2,1,0:T(8,128)(2,1)S(1)}, u32[]{:S(2)}, u32[]{:S(2)}) async-start(bf16[4,192,128]{2,1,0:T(8,128)(2,1)} %get-tuple-element.111), calls=%async_computation.5 | async-start | bytes 393216 | tf_op jit(solution)/shard_map/all_to_all | solution.py:711
  175.0 3.3 %add_convert_fusion.1 = bf16[768,768]{1,0:T(8,128)(2,1)} fusion(bf16[768,768]{1,0:T(8,128)(2,1)} %collective-permute-done.7, bf16[512,768]{1,0:T(8,128)(2,1)S(1)} %bitcast.155, bf16[512,3072]{1,0:T(8,128)(2,1)} %get-tuple-element.152), kind=kOutput, calls=%fused_computation.4 | convolution fusion | flops 605749248 | bytes 3932160 | tf_op jit(solution)/shard_map/dot_general | solution.py:30
  178.3 3.2 %side_grad.1 = f32[8,96,896]{2,1,0:T(8,128)} custom-call(bf16[4,192,128]{2,1,0:T(8,128)(2,1)} %copy-done.11, bf16[128,768]{1,0:T(8,128)(2,1)} %get-tuple-element.113.grad_ref, f32[768,128]{1,0:T(8,128)} %get-tuple-element.114.router_ref), custom_call_target="tpu_custom_call" | custom-call | bytes 170000 | tf_op jit(solution)/shard_map/side_grad/pallas_call | solution.py:611
  182.3 5.1 %all-to-all-start.6 = ((bf16[8,64,768]{2,1,0:T(8,128)(2,1)}), bf16[8,64,768]{2,1,0:T(8,128)(2,1)}, u32[]{:S(2)}, u32[]{:S(2)}) async-start(bf16[8,64,768]{2,1,0:T(8,128)(2,1)} %bitcast.44), calls=%async_computation.6 | async-start | bytes 1572864 | tf_op jit(solution)/shard_map/all_to_all | solution.py:711
  188.6 9.4 %attention_backward.2 = (f32[4,128,192]{2,1,0:T(8,128)}, bf16[1,4,128,384]{3,2,1,0:T(8,128)(2,1)}, f32[1,3,5,256]{3,2,1,0:T(8,128)}) custom-call(s32[4]{0:T(128)} %get-tuple-element.213.place_ref, bf16[4,128,192]{2,1,0:T(8,128)(2,1)} %get-tuple-element.92.q_ref, bf16[1,4,128,384]{3,2,1,0:T(8,128)(2,1)} %bitcast.172, s32[4,128,1]{2,1,0:T(8,128)} %copy.54.refs_2_.start_ref, ...), custom_call_target="tpu_custom_call" | custom-call | bytes 27200000 | tf_op jit(solution)/shard_map/attention_backward/pallas_call | solution.py:313
  200.7 9.5 %attention_backward.3 = (f32[4,128,192]{2,1,0:T(8,128)}, f32[1,4,128,384]{3,2,1,0:T(8,128)}, f32[1,3,5,256]{3,2,1,0:T(8,128)}) custom-call(s32[4]{0:T(128)} %get-tuple-element.212.place_ref, bf16[4,128,192]{2,1,0:T(8,128)(2,1)} %get-tuple-element.92.q_ref, bf16[1,4,128,384]{3,2,1,0:T(8,128)(2,1)} %bitcast.171, s32[4,128,1]{2,1,0:T(8,128)} %copy.54.refs_2_.start_ref, ...), custom_call_target="tpu_custom_call" | custom-call | bytes 3400000 | tf_op jit(solution)/shard_map/attention_backward/pallas_call | solution.py:313
  210.2 4.3 %collective-permute-done.10 = bf16[768,768]{1,0:T(8,128)(2,1)} collective-permute-done((bf16[768,768]{1,0:T(8,128)(2,1)}, bf16[768,768]{1,0:T(8,128)(2,1)}, u32[]{:S(2)}, u32[]{:S(2)}) %collective-permute-start.10) | collective-permute-done | bytes 1179680 | tf_op jit(solution)/shard_map/ppermute | solution.py:694
  214.5 4.4 %project_back.1 = (bf16[512,576]{1,0:T(8,128)(2,1)}, f32[1,768]{1,0:T(1,128)}, bf16[4,128,768]{2,1,0:T(8,128)(2,1)}) custom-call(f32[4,128,192]{2,1,0:T(8,128)} %get-tuple-element.124.dq_ref, f32[4,128,192]{2,1,0:T(8,128)} %get-tuple-element.125.dq_other_ref, f32[4,128,384]{2,1,0:T(8,128)} %bitcast.175, ...), custom_call_target="tpu_custom_call" | custom-call | bytes 13600000 | tf_op jit(solution)/shard_map/project_back/pallas_call | solution.py:566
  224.6 3.4 %qkv_grad.1 = f32[8,96,576]{2,1,0:T(8,128)} custom-call(bf16[4,128,768]{2,1,0:T(8,128)(2,1)} %get-tuple-element.128.h_ref, bf16[512,576]{1,0:T(8,128)(2,1)} %get-tuple-element.134.dproj_ref), custom_call_target="tpu_custom_call" | custom-call | bytes 170000 | tf_op jit(solution)/shard_map/qkv_grad/pallas_call | solution.py:589
  230.8 4.8 %all-to-all-start.7 = ((bf16[4,128,768]{2,1,0:T(8,128)(2,1)}), bf16[4,128,768]{2,1,0:T(8,128)(2,1)}, u32[]{:S(2)}, u32[]{:S(2)}) async-start(bf16[4,128,768]{2,1,0:T(8,128)(2,1)} %get-tuple-element.140), calls=%async_computation.7 | async-start | bytes 1572864 | tf_op jit(solution)/shard_map/all_to_all | solution.py:711
  249.6 4.3 %collective-permute-done.14 = bf16[8,24,1472]{2,1,0:T(8,128)(2,1)} collective-permute-done((bf16[8,24,1472]{2,1,0:T(8,128)(2,1)}, bf16[8,24,1472]{2,1,0:T(8,128)(2,1)}, u32[]{:S(2)}, u32[]{:S(2)}) %collective-permute-start.14) | collective-permute-done | bytes 565280 | tf_op jit(solution)/shard_map/ppermute | solution.py:694
  260.3 3.1 %add_bitcast_fusion = f32[1,768,768]{2,1,0:T(8,128)} fusion(bf16[768,768]{1,0:T(8,128)(2,1)S(1)} %copy-done.17, f32[768,768]{1,0:T(8,128)S(1)} %fusion.3, bf16[768,768]{1,0:T(8,128)(2,1)} %collective-permute-done.15), kind=kLoop, calls=%fused_computation.1 | loop fusion | flops 2359296 | bytes 7077888 | tf_op jit(solution)/shard_map/broadcast_in_dim | solution.py:985
  272.9 3.4 %add_bitcast_fusion.1 = f32[1,768,768]{2,1,0:T(8,128)} fusion(bf16[768,768]{1,0:T(8,128)(2,1)} %collective-permute-done.10, f32[768,768]{1,0:T(8,128)S(1)} %fusion.5, bf16[768,768]{1,0:T(8,128)(2,1)} %collective-permute-done.16), kind=kLoop, calls=%fused_computation.2 | loop fusion | flops 2359296 | bytes 7077888 | tf_op jit(solution)/shard_map/broadcast_in_dim | solution.py:984
  281.3 3.5 %collective-permute-done.22 = bf16[24,3456]{1,0:T(8,128)(2,1)S(1)} collective-permute-done((bf16[24,3456]{1,0:T(8,128)(2,1)}, bf16[24,3456]{1,0:T(8,128)(2,1)S(1)}, u32[]{:S(2)}, u32[]{:S(2)}) %collective-permute-start.22) | collective-permute-done | bytes 165920 | tf_op jit(solution)/shard_map/ppermute | solution.py:694
  (218 shorter events, 100.6 us)
Async XLA Ops:
  3.0 20.8 %collective-permute-start = (bf16[128,768]{1,0:T(8,128)(2,1)S(1)}, bf16[128,768]{1,0:T(8,128)(2,1)S(1)}, u32[]{:S(2)}, u32[]{:S(2)}) collective-permute-start(bf16[128,768]{1,0:T(8,128)(2,1)S(1)} %multiply_convert_fusion.h0_ref), channel_id=1, source_target_pairs={{0,2},{2,4},{4,6},{6,0},{1,3},{3,5},{5,7},{7,1},{8,10},{10,12},{12... | collective-permute-start | bytes 589832 | tf_op jit(solution)/shard_map/ppermute | solution.py:702
  6.1 17.7 %collective-permute-start.1 = (bf16[128,768]{1,0:T(8,128)(2,1)S(1)}, bf16[128,768]{1,0:T(8,128)(2,1)S(1)}, u32[]{:S(2)}, u32[]{:S(2)}) collective-permute-start(bf16[128,768]{1,0:T(8,128)(2,1)S(1)} %multiply_convert_fusion.h0_ref), channel_id=1, source_target_pairs={{0,4},{2,6},{4,0},{6,2},{1,5},{3,7},{5,1},{7,3},{8,12},{10,14},{12... | collective-permute-start | bytes 589832 | tf_op jit(solution)/shard_map/ppermute | solution.py:702
  8.7 15.1 %collective-permute-start.2 = (bf16[128,768]{1,0:T(8,128)(2,1)S(1)}, bf16[128,768]{1,0:T(8,128)(2,1)S(1)}, u32[]{:S(2)}, u32[]{:S(2)}) collective-permute-start(bf16[128,768]{1,0:T(8,128)(2,1)S(1)} %multiply_convert_fusion.h0_ref), channel_id=1, source_target_pairs={{0,6},{2,0},{4,2},{6,4},{1,7},{3,1},{5,3},{7,5},{8,14},{10,8},{12,... | collective-permute-start | bytes 589832 | tf_op jit(solution)/shard_map/ppermute | solution.py:702
  12.2 24.1 %all-to-all-start = ((bf16[8,48,576]{2,1,0:T(8,128)(2,1)}), bf16[8,48,576]{2,1,0:T(8,128)(2,1)S(1)}, u32[]{:S(2)}, u32[]{:S(2)}) async-start(bf16[8,48,576]{2,1,0:T(8,128)(2,1)} %reshape.156), calls=%async_computation | async-start | bytes 983040 | tf_op jit(solution)/shard_map/all_to_all | solution.py:711
  36.3 37.1 %all-to-all-start.1 = ((bf16[8,88,896]{2,1,0:T(8,128)(2,1)}), bf16[8,88,896]{2,1,0:T(8,128)(2,1)S(1)}, u32[]{:S(2)}, u32[]{:S(2)}) async-start(bf16[8,88,896]{2,1,0:T(8,128)(2,1)} %pad_maximum_fusion.1), calls=%async_computation.1 | async-start | bytes 2523136 | tf_op jit(solution)/shard_map/all_to_all | solution.py:711
  40.1 1.9 collective-permute-start.3
  46.7 18.6 %collective-permute-start.4 = (bf16[4,128,384]{2,1,0:T(8,128)(2,1)}, bf16[4,128,384]{2,1,0:T(8,128)(2,1)S(1)}, u32[]{:S(2)}, u32[]{:S(2)}) collective-permute-start(bf16[4,128,384]{2,1,0:T(8,128)(2,1)} %get-tuple-element.93.refs_0_), channel_id=1, source_target_pairs={{0,1},{1,0},{2,3},{3,2},{4,5},{5,4},{6,7},{7,6},{8,9},{9,8},{10,11... | collective-permute-start | bytes 1179656 | tf_op jit(solution)/shard_map/ppermute | solution.py:694
  73.4 10.0 %collective-permute-start.5 = (bf16[8,24,896]{2,1,0:T(8,128)(2,1)S(1)}, bf16[8,24,896]{2,1,0:T(8,128)(2,1)S(1)}, u32[]{:S(2)}, u32[]{:S(2)}) collective-permute-start(bf16[8,24,896]{2,1,0:T(8,128)(2,1)S(1)} %get-tuple-element.199), channel_id=1, source_target_pairs={{0,16},{16,0},{1,17},{17,1},{2,18},{18,2},{3,19},{19,3},{4,20},{20... | collective-permute-start | bytes 1032200 | tf_op jit(solution)/shard_map/ppermute | solution.py:694
  75.0 13.6 %all-to-all-start.2 = ((bf16[4,192,128]{2,1,0:T(8,128)(2,1)}), bf16[4,192,128]{2,1,0:T(8,128)(2,1)S(1)}, u32[]{:S(2)}, u32[]{:S(2)}) async-start(bf16[4,192,128]{2,1,0:T(8,128)(2,1)} %get-tuple-element.98), calls=%async_computation.2 | async-start | bytes 393216 | tf_op jit(solution)/shard_map/all_to_all | solution.py:711
  88.6 2.1 collective-permute-start.6
  95.3 24.2 %all-to-all-start.3 = ((bf16[8,64,768]{2,1,0:T(8,128)(2,1)}), bf16[8,64,768]{2,1,0:T(8,128)(2,1)S(1)}, u32[]{:S(2)}, u32[]{:S(2)}) async-start(bf16[8,64,768]{2,1,0:T(8,128)(2,1)} %bitcast.174), calls=%async_computation.3 | async-start | bytes 1572864 | tf_op jit(solution)/shard_map/all_to_all | solution.py:711
  142.7 12.1 %collective-permute-start.8 = (bf16[768,768]{1,0:T(8,128)(2,1)}, bf16[768,768]{1,0:T(8,128)(2,1)S(1)}, u32[]{:S(2)}, u32[]{:S(2)}) collective-permute-start(bf16[768,768]{1,0:T(8,128)(2,1)} %convolution_convert_fusion), channel_id=1, source_target_pairs={{0,8},{8,0},{1,9},{9,1},{2,10},{10,2},{3,11},{11,3},{4,12},{12,4},... | collective-permute-start | bytes 3538952 | tf_op jit(solution)/shard_map/ppermute | solution.py:694
  142.7 24.6 %all-to-all-start.4 = ((bf16[8,64,768]{2,1,0:T(8,128)(2,1)}), bf16[8,64,768]{2,1,0:T(8,128)(2,1)S(1)}, u32[]{:S(2)}, u32[]{:S(2)}) async-start(bf16[8,64,768]{2,1,0:T(8,128)(2,1)} %bitcast.40), calls=%async_computation.4 | async-start | bytes 1572864 | tf_op jit(solution)/shard_map/all_to_all | solution.py:711
  149.5 25.4 %collective-permute-start.7 = (bf16[768,768]{1,0:T(8,128)(2,1)}, bf16[768,768]{1,0:T(8,128)(2,1)}, u32[]{:S(2)}, u32[]{:S(2)}) collective-permute-start(bf16[768,768]{1,0:T(8,128)(2,1)} %convolution_convert_fusion.1), channel_id=1, source_target_pairs={{0,8},{8,0},{1,9},{9,1},{2,10},{10,2},{3,11},{11,3},{4,12},{12,4},... | collective-permute-start | bytes 3538952 | tf_op jit(solution)/shard_map/ppermute | solution.py:694
  156.6 41.3 %collective-permute-start.9 = (bf16[768,768]{1,0:T(8,128)(2,1)}, bf16[768,768]{1,0:T(8,128)(2,1)S(1)}, u32[]{:S(2)}, u32[]{:S(2)}) collective-permute-start(bf16[768,768]{1,0:T(8,128)(2,1)} %add_convert_fusion), channel_id=1, source_target_pairs={{0,16},{16,0},{1,17},{17,1},{2,18},{18,2},{3,19},{19,3},{4,20},{20... | collective-permute-start | bytes 3538952 | tf_op jit(solution)/shard_map/ppermute | solution.py:694
  171.6 10.7 %all-to-all-start.5 = ((bf16[4,192,128]{2,1,0:T(8,128)(2,1)}), bf16[4,192,128]{2,1,0:T(8,128)(2,1)S(1)}, u32[]{:S(2)}, u32[]{:S(2)}) async-start(bf16[4,192,128]{2,1,0:T(8,128)(2,1)} %get-tuple-element.111), calls=%async_computation.5 | async-start | bytes 393216 | tf_op jit(solution)/shard_map/all_to_all | solution.py:711
  182.3 32.2 %all-to-all-start.6 = ((bf16[8,64,768]{2,1,0:T(8,128)(2,1)}), bf16[8,64,768]{2,1,0:T(8,128)(2,1)}, u32[]{:S(2)}, u32[]{:S(2)}) async-start(bf16[8,64,768]{2,1,0:T(8,128)(2,1)} %bitcast.44), calls=%async_computation.6 | async-start | bytes 1572864 | tf_op jit(solution)/shard_map/all_to_all | solution.py:711
  187.4 27.1 %collective-permute-start.10 = (bf16[768,768]{1,0:T(8,128)(2,1)}, bf16[768,768]{1,0:T(8,128)(2,1)}, u32[]{:S(2)}, u32[]{:S(2)}) collective-permute-start(bf16[768,768]{1,0:T(8,128)(2,1)} %add_convert_fusion.1), channel_id=1, source_target_pairs={{0,16},{16,0},{1,17},{17,1},{2,18},{18,2},{3,19},{19,3},{4,20},{20... | collective-permute-start | bytes 3538952 | tf_op jit(solution)/shard_map/ppermute | solution.py:694
  198.0 16.5 %collective-permute-start.11 = (bf16[4,128,384]{2,1,0:T(8,128)(2,1)}, bf16[4,128,384]{2,1,0:T(8,128)(2,1)}, u32[]{:S(2)}, u32[]{:S(2)}) collective-permute-start(bf16[4,128,384]{2,1,0:T(8,128)(2,1)} %bitcast.193), channel_id=1, source_target_pairs={{0,1},{1,0},{2,3},{3,2},{4,5},{5,4},{6,7},{7,6},{8,9},{9,8},{10,11... | collective-permute-start | bytes 1179656 | tf_op jit(solution)/shard_map/ppermute | solution.py:694
  219.9 2.5 collective-permute-start.12
  229.5 6.2 %collective-permute-start.13 = (bf16[8,48,576]{2,1,0:T(8,128)(2,1)S(1)}, bf16[8,48,576]{2,1,0:T(8,128)(2,1)}, u32[]{:S(2)}, u32[]{:S(2)}) collective-permute-start(bf16[8,48,576]{2,1,0:T(8,128)(2,1)S(1)} %fusion.22), channel_id=1, source_target_pairs={{0,8},{8,0},{1,9},{9,1},{2,10},{10,2},{3,11},{11,3},{4,12},{12,4},... | collective-permute-start | bytes 1327112 | tf_op jit(solution)/shard_map/ppermute | solution.py:694
  229.7 26.5 %collective-permute-start.15 = (bf16[768,768]{1,0:T(8,128)(2,1)}, bf16[768,768]{1,0:T(8,128)(2,1)}, u32[]{:S(2)}, u32[]{:S(2)}) collective-permute-start(bf16[768,768]{1,0:T(8,128)(2,1)} %convolution_convert_fusion.3), channel_id=1, source_target_pairs={{0,8},{8,0},{1,9},{9,1},{2,10},{10,2},{3,11},{11,3},{4,12},{12,4},... | collective-permute-start | bytes 3538952 | tf_op jit(solution)/shard_map/ppermute | solution.py:694
  230.0 26.1 %collective-permute-start.16 = (bf16[768,768]{1,0:T(8,128)(2,1)}, bf16[768,768]{1,0:T(8,128)(2,1)}, u32[]{:S(2)}, u32[]{:S(2)}) collective-permute-start(bf16[768,768]{1,0:T(8,128)(2,1)} %convolution_convert_fusion.2), channel_id=1, source_target_pairs={{0,8},{8,0},{1,9},{9,1},{2,10},{10,2},{3,11},{11,3},{4,12},{12,4},... | collective-permute-start | bytes 3538952 | tf_op jit(solution)/shard_map/ppermute | solution.py:694
  230.8 25.5 %all-to-all-start.7 = ((bf16[4,128,768]{2,1,0:T(8,128)(2,1)}), bf16[4,128,768]{2,1,0:T(8,128)(2,1)}, u32[]{:S(2)}, u32[]{:S(2)}) async-start(bf16[4,128,768]{2,1,0:T(8,128)(2,1)} %get-tuple-element.140), calls=%async_computation.7 | async-start | bytes 1572864 | tf_op jit(solution)/shard_map/all_to_all | solution.py:711
  238.3 15.6 %collective-permute-start.14 = (bf16[8,24,1472]{2,1,0:T(8,128)(2,1)}, bf16[8,24,1472]{2,1,0:T(8,128)(2,1)}, u32[]{:S(2)}, u32[]{:S(2)}) collective-permute-start(bf16[8,24,1472]{2,1,0:T(8,128)(2,1)} %fusion.20), channel_id=1, source_target_pairs={{0,16},{16,0},{1,17},{17,1},{2,18},{18,2},{3,19},{19,3},{4,20},{20... | collective-permute-start | bytes 1695752 | tf_op jit(solution)/shard_map/ppermute | solution.py:694
  245.9 3.8 %collective-permute-start.18 = (f32[24,128]{1,0:T(8,128)S(1)}, f32[24,128]{1,0:T(8,128)S(1)}, u32[]{:S(2)}, u32[]{:S(2)}) collective-permute-start(f32[24,128]{1,0:T(8,128)S(1)} %pad.28), channel_id=1, source_target_pairs={{0,1},{1,0},{2,3},{3,2},{4,5},{5,4},{6,7},{7,6},{8,9},{9,8},{10,11... | collective-permute-start | bytes 36872 | tf_op jit(solution)/shard_map/ppermute | solution.py:694
  258.7 8.2 %collective-permute-start.17 = (bf16[4,24,1472]{2,1,0:T(8,128)(2,1)S(1)}, bf16[4,24,1472]{2,1,0:T(8,128)(2,1)S(1)}, u32[]{:S(2)}, u32[]{:S(2)}) collective-permute-start(bf16[4,24,1472]{2,1,0:T(8,128)(2,1)S(1)} %fusion.23), channel_id=1, source_target_pairs={{0,1},{1,0},{2,3},{3,2},{4,5},{5,4},{6,7},{7,6},{8,9},{9,8},{10,11... | collective-permute-start | bytes 847880 | tf_op jit(solution)/shard_map/ppermute | solution.py:694
  267.8 8.6 %collective-permute-start.19 = (bf16[24,1728]{1,0:T(8,128)(2,1)S(1)}, bf16[24,1728]{1,0:T(8,128)(2,1)S(1)}, u32[]{:S(2)}, u32[]{:S(2)}) collective-permute-start(bf16[24,1728]{1,0:T(8,128)(2,1)S(1)} %get-tuple-element.202), channel_id=1, source_target_pairs={{0,2},{2,4},{4,6},{6,0},{1,3},{3,5},{5,7},{7,1},{8,10},{10,12},{12... | collective-permute-start | bytes 248840 | tf_op jit(solution)/shard_map/ppermute | solution.py:702
  269.1 7.7 %collective-permute-start.20 = (bf16[24,1728]{1,0:T(8,128)(2,1)S(1)}, bf16[24,1728]{1,0:T(8,128)(2,1)S(1)}, u32[]{:S(2)}, u32[]{:S(2)}) collective-permute-start(bf16[24,1728]{1,0:T(8,128)(2,1)S(1)} %get-tuple-element.203), channel_id=1, source_target_pairs={{0,4},{2,6},{4,0},{6,2},{1,5},{3,7},{5,1},{7,3},{8,12},{10,14},{12... | collective-permute-start | bytes 248840 | tf_op jit(solution)/shard_map/ppermute | solution.py:702
  271.4 5.4 %collective-permute-start.21 = (bf16[24,1728]{1,0:T(8,128)(2,1)S(1)}, bf16[24,1728]{1,0:T(8,128)(2,1)S(1)}, u32[]{:S(2)}, u32[]{:S(2)}) collective-permute-start(bf16[24,1728]{1,0:T(8,128)(2,1)S(1)} %get-tuple-element.200), channel_id=1, source_target_pairs={{0,6},{2,0},{4,2},{6,4},{1,7},{3,1},{5,3},{7,5},{8,14},{10,8},{12,... | collective-permute-start | bytes 248840 | tf_op jit(solution)/shard_map/ppermute | solution.py:702
  279.2 5.6 %collective-permute-start.22 = (bf16[24,3456]{1,0:T(8,128)(2,1)}, bf16[24,3456]{1,0:T(8,128)(2,1)S(1)}, u32[]{:S(2)}, u32[]{:S(2)}) collective-permute-start(bf16[24,3456]{1,0:T(8,128)(2,1)} %assemble.1), channel_id=1, source_target_pairs={{0,16},{16,0},{1,17},{17,1},{2,18},{18,2},{3,19},{19,3},{4,20},{20... | collective-permute-start | bytes 497672 | tf_op jit(solution)/shard_map/ppermute | solution.py:694
  285.9 1.7 collective-permute-start.23
  (42 other events, 267.2 us)
where the time goes:
time: 296 us; the launch traced here: 295 us
  waiting for transfers between devices  84.7 us (29%)
  Pallas kernels  73.3 us (25%)
  starting transfers between devices  58.5 us (20%)
  local copies, waits for them, and re-layouts  26.3 us (9%)
  other arithmetic  25.5 us (9%)
  matrix products  25.1 us (8%)
    all_to_all x8, waiting for transfers between devices, exchange(): return lax.all_to_all(value, axes, split_axis=0, concat_axis=0, tiled=True)  46.6 us
    ppermute x18, waiting for transfers between devices, swap(): return lax.ppermute(value, axis, [(0, 1), (1, 0)])  37.6 us
    all_to_all x8, starting transfers between devices, exchange(): return lax.all_to_all(value, axes, split_axis=0, concat_axis=0, tiled=True)  34.2 us
    dot_general x9, matrix products, dotf(): return lax.dot_general(a, b, dims, preferred_element_type=F32)  22.9 us
    pallas_call x1, Pallas kernels, expert_layer(): pl.pallas_call(expert_kernel, grid_spec=pltpu.PrefetchScalarGridSpec(num_...  19 us
    pallas_call x2, Pallas kernels, attention_backward(): pl.pallas_call(backward_kernel, in_specs=[SM] + [VM] * 7, out_specs=[VM]...  18.9 us
    ppermute x6, starting transfers between devices, turn(): lax.ppermute(value, 'g', [(j, (j + step) % GROUPS) for j in range(GROUPS)])  12.2 us
    ppermute x18, starting transfers between devices, swap(): return lax.ppermute(value, axis, [(0, 1), (1, 0)])  12.1 us
  transfers between devices with their start and end apart: 32, of which 17 were waited for; matrix products, arithmetic and copies ran while one was open for 18% of the time, Pallas kernels for 13%

commit v1 on v0

--- a/solution.py
+++ b/solution.py
@@ -876,6 +876,7 @@
     side_grad = side_grad_of(att, attn_grad, router_grad, ranks)
     out_grad, produced, side_grad, away_in = tie(out_grad, produced, side_grad, away[1])
     far_in = swap(away_in, "y")
+    side_grad = halve(side_grad, c, "c")
     near = [swap(grad, "c") for grad in near]
     returned = exchange(produced.reshape(ranks, capacity, D), SEQ)
 
@@ -899,7 +900,9 @@
             BF,
             8,
         )
-        out_grad, dq_other, dkv_other, far_out = tie(out_grad, dq_other, dkv_other, far_out)
+        out_grad, dq_other, dkv_other, far_out, side_grad = tie(
+            out_grad, dq_other, dkv_other, far_out, side_grad
+        )
         dkv_came = swap(dkv_other[0], "i")
         dq, dkv_own, dist = attention_backward(
             place_of(i[None]),
@@ -923,21 +926,17 @@
         dkv_came = jnp.zeros(dkv_own.shape, BF)
         dq_other = jnp.zeros_like(dq)
         dist = jnp.take(dist, (i - jnp.arange(inner)) % inner, axis=0)
-    dkv_own, returned, far_in = tie(dkv_own, returned, far_in)
+    dkv_own, returned, far_in, side_grad = tie(dkv_own, returned, far_in, side_grad)
+    side_grad = halve(side_grad, y, "y")
     returned = returned.reshape(ranks * capacity, D)
     dproj, gain_one, half = project_back(
         dq, dq_other, dkv_own, dkv_came, w_cols, h_col, gain_attn[None]
     )
     half = exchange(half, "g")
-    dproj, side_grad = tie(dproj, side_grad)
-    side_grad = halve(side_grad, c, "c")
-    dproj, side_grad = tie(dproj, side_grad)
     parts = halve(qkv_grad_of(h_col, dproj, ranks), c, "c")
-    parts, gain_one, gain_two, dist = tie(
-        jnp.concatenate((side_grad, parts), axis=2), gain_one, gain_two, dist
-    )
-    parts = halve(parts, y, "y")
-    parts, half, active, hidden_grad, *near = tie(parts, half, active, hidden_grad, *near)
+    parts, gain_one, gain_two, dist = tie(parts, gain_one, gain_two, dist)
+    parts = jnp.concatenate((side_grad, halve(parts, y, "y")), axis=2)
+    parts, active, hidden_grad, *near = tie(parts, active, hidden_grad, *near)
     mine_out, mine_in = [
         grad + core.astype(F32) for grad, core in zip(part_grads(3, active, hidden_grad), near)
     ]
@@ -959,7 +958,7 @@
     small = jnp.concatenate((high, small - high), axis=1).astype(BF)
     small = jnp.broadcast_to(small[None], (groups, rows, 2 * width))
 
-    parts = jnp.concatenate((inner_reduce(parts), small), axis=2)
+    parts, half = tie(jnp.concatenate((inner_reduce(parts), small), axis=2), half)
     parts = [pick(parts, g, 0)] + [
         turn(pick(parts, lax.rem(g + step, groups), 0), step) for step in range(1, groups)
     ]

time: 296 us -> 289 us (0.976)
  other arithmetic: 25.5 us -> 19.8 us
  waiting for transfers between devices: 84.7 us -> 81.5 us
    ppermute x18 -> x19, waiting for transfers between devices: 37.6 us -> 35.6 us  [swap(): return lax.ppermute(value, axis, [(0, 1), (1, 0)])]
    ppermute x18 -> x19, starting transfers between devices: 12.1 us -> 13.5 us  [swap(): return lax.ppermute(value, axis, [(0, 1), (1, 0)])]
    unnamed x86 -> x82, local copies, waits for them, and re-layouts: 5.88 us -> 6.33 us
  transfers between devices with their start and end apart: 32 -> 33, of which waited for: 17 -> 15; matrix products, arithmetic and copies ran while one was open for 18% -> 19% of each run, Pallas kernels for 13% -> 16%
where the time goes in v1:
time: 289 us; the launch traced here: 287 us
  waiting for transfers between devices  81.5 us (28%)
  Pallas kernels  73.6 us (25%)
  starting transfers between devices  59.8 us (21%)
  matrix products  26.5 us (9%)
  local copies, waits for them, and re-layouts  24.7 us (9%)
  other arithmetic  19.8 us (7%)
    all_to_all x8, waiting for transfers between devices, exchange(): return lax.all_to_all(value, axes, split_axis=0, concat_axis=0, tiled=True)  45.9 us
    ppermute x19, waiting for transfers between devices, swap(): return lax.ppermute(value, axis, [(0, 1), (1, 0)])  35.6 us
    all_to_all x8, starting transfers between devices, exchange(): return lax.all_to_all(value, axes, split_axis=0, concat_axis=0, tiled=True)  34 us
    dot_general x9, matrix products, dotf(): return lax.dot_general(a, b, dims, preferred_element_type=F32)  25 us
    pallas_call x1, Pallas kernels, expert_layer(): pl.pallas_call(expert_kernel, grid_spec=pltpu.PrefetchScalarGridSpec(num_...  19.2 us
    pallas_call x2, Pallas kernels, attention_backward(): pl.pallas_call(backward_kernel, in_specs=[SM] + [VM] * 7, out_specs=[VM]...  18.9 us
    ppermute x19, starting transfers between devices, swap(): return lax.ppermute(value, axis, [(0, 1), (1, 0)])  13.5 us
    ppermute x6, starting transfers between devices, turn(): lax.ppermute(value, 'g', [(j, (j + step) % GROUPS) for j in range(GROUPS)])  12.3 us
  transfers between devices with their start and end apart: 33, of which 15 were waited for; matrix products, arithmetic and copies ran while one was open for 19% of the time, Pallas kernels for 16%

profile of v1, /device:TPU:0, one launch (start us, length us, event | category | flops | bytes accessed | tf_op | source)
XLA Modules:
  0.0 287.3 jit_solution(12900370931054913276)
XLA Ops:
  12.2 3.5 %all-to-all-start = ((bf16[8,48,576]{2,1,0:T(8,128)(2,1)}), bf16[8,48,576]{2,1,0:T(8,128)(2,1)S(1)}, u32[]{:S(2)}, u32[]{:S(2)}) async-start(bf16[8,48,576]{2,1,0:T(8,128)(2,1)} %reshape.160), calls=%async_computation | async-start | bytes 983040 | tf_op jit(solution)/shard_map/all_to_all | solution.py:711
  23.8 12.5 %all-to-all-done = bf16[8,48,576]{2,1,0:T(8,128)(2,1)S(1)} async-done(((bf16[8,48,576]{2,1,0:T(8,128)(2,1)}), bf16[8,48,576]{2,1,0:T(8,128)(2,1)S(1)}, u32[]{:S(2)}, u32[]{:S(2)}) %all-to-all-start) | async-done | bytes 442400 | tf_op jit(solution)/shard_map/all_to_all | solution.py:711
  36.3 3.8 %all-to-all-start.1 = ((bf16[8,88,896]{2,1,0:T(8,128)(2,1)}), bf16[8,88,896]{2,1,0:T(8,128)(2,1)S(1)}, u32[]{:S(2)}, u32[]{:S(2)}) async-start(bf16[8,88,896]{2,1,0:T(8,128)(2,1)} %pad_maximum_fusion), calls=%async_computation.1 | async-start | bytes 2523136 | tf_op jit(solution)/shard_map/all_to_all | solution.py:711
  43.3 3.5 %project.1 = (bf16[4,128,192]{2,1,0:T(8,128)(2,1)}, bf16[4,128,384]{2,1,0:T(8,128)(2,1)}, bf16[4,128,768]{2,1,0:T(8,128)(2,1)}) custom-call(s32[1]{0:T(128)} %bitcast.2.own_ref, bf16[128,768]{1,0:T(8,128)(2,1)} %copy-done.15, bf16[128,768]{1,0:T(8,128)(2,1)} %copy-done.24, bf16[128,768]{1,0:T(8,128)(2,1)} %copy-done.25, bf16[128,768]{1,0:T(8,128)(2,1)} %copy-done.26, ...), custom_call_target="tpu_custom_call" | custom-call | bytes 170000 | tf_op jit(solution)/shard_map/project/pallas_call | solution.py:345
  50.2 15.2 %collective-permute-done.4.refs_1_ = bf16[4,128,384]{2,1,0:T(8,128)(2,1)S(1)} collective-permute-done((bf16[4,128,384]{2,1,0:T(8,128)(2,1)}, bf16[4,128,384]{2,1,0:T(8,128)(2,1)S(1)}, u32[]{:S(2)}, u32[]{:S(2)}) %collective-permute-start.4) | collective-permute-done | bytes 393248 | tf_op jit(solution)/shard_map/ppermute | solution.py:694
  66.1 7.2 %attention_forward.1 = (bf16[4,192,128]{2,1,0:T(8,128)(2,1)}, f32[4,128,192]{2,1,0:T(8,128)}, f32[4,384,128]{2,1,0:T(8,128)}) custom-call(s32[5]{0:T(128)} %concatenate.44.place_ref, bf16[4,128,192]{2,1,0:T(8,128)(2,1)} %get-tuple-element.91.q_ref, bf16[4,128,384]{2,1,0:T(8,128)(2,1)} %get-tuple-element.92.refs_0_, bf16[4,128,384]{2,1,0:T(8,128)(2,1)} %copy-done.13, ...), custom_call_target="tpu_custom_call" | custom-call | bytes 23800000 | tf_op jit(solution)/shard_map/attention_forward/pallas_call | solution.py:201
  75.0 6.3 %all-to-all-start.2 = ((bf16[4,192,128]{2,1,0:T(8,128)(2,1)}), bf16[4,192,128]{2,1,0:T(8,128)(2,1)S(1)}, u32[]{:S(2)}, u32[]{:S(2)}) async-start(bf16[4,192,128]{2,1,0:T(8,128)(2,1)} %get-tuple-element.97), calls=%async_computation.2 | async-start | bytes 393216 | tf_op jit(solution)/shard_map/all_to_all | solution.py:711
  83.6 5.0 %all-to-all-done.2.att_ref = bf16[4,192,128]{2,1,0:T(8,128)(2,1)S(1)} async-done(((bf16[4,192,128]{2,1,0:T(8,128)(2,1)}), bf16[4,192,128]{2,1,0:T(8,128)(2,1)S(1)}, u32[]{:S(2)}, u32[]{:S(2)}) %all-to-all-start.2) | async-done | bytes 196640 | tf_op jit(solution)/shard_map/all_to_all | solution.py:711
  92.0 3.3 %mlp_in.1 = (f32[128,768]{1,0:T(8,128)}, bf16[512,768]{1,0:T(8,128)(2,1)}) custom-call(bf16[4,192,128]{2,1,0:T(8,128)(2,1)} %copy-done.10, bf16[4,192,768]{2,1,0:T(8,128)(2,1)} %bitcast.152, f32[128,768]{1,0:T(8,128)} %bitcast.154, f32[1,768]{1,0:T(1,128)} %broadcast_in_dim.37.gain_ref, bf16[512,128]{1,0:T(8,128)(2,1)} %get-tuple-element.208.disp_ref), custom_call_target="tpu_custom_call" | custom-call | bytes 170000 | tf_op jit(solution)/shard_map/mlp_in/pallas_call | solution.py:372
  95.3 3.7 %all-to-all-start.3 = ((bf16[8,64,768]{2,1,0:T(8,128)(2,1)}), bf16[8,64,768]{2,1,0:T(8,128)(2,1)S(1)}, u32[]{:S(2)}, u32[]{:S(2)}) async-start(bf16[8,64,768]{2,1,0:T(8,128)(2,1)} %bitcast.185), calls=%async_computation.3 | async-start | bytes 1572864 | tf_op jit(solution)/shard_map/all_to_all | solution.py:711
  101.5 18.1 %all-to-all-done.3 = bf16[8,64,768]{2,1,0:T(8,128)(2,1)S(1)} async-done(((bf16[8,64,768]{2,1,0:T(8,128)(2,1)}), bf16[8,64,768]{2,1,0:T(8,128)(2,1)S(1)}, u32[]{:S(2)}, u32[]{:S(2)}) %all-to-all-start.3) | async-done | bytes 786464 | tf_op jit(solution)/shard_map/all_to_all | solution.py:711
  120.4 19.2 %expert_layer.1 = (bf16[512,3072]{1,0:T(8,128)(2,1)}, bf16[512,3072]{1,0:T(8,128)(2,1)}, bf16[512,768]{1,0:T(8,128)(2,1)}, bf16[512,768]{1,0:T(8,128)(2,1)}, bf1...) custom-call(s32[5]{0:T(128)} %stack.101.own_ref, bf16[512,768]{1,0:T(8,128)(2,1)} %bitcast.159, bf16[512,896]{1,0:T(8,128)(2,1)} %bitcast.172, ...), custom_call_target="tpu_custom_call" | custom-call | bytes 170000 | tf_op jit(solution)/shard_map/expert_layer/pallas_call | solution.py:464
  139.6 3.3 %convolution_convert_fusion = bf16[768,768]{1,0:T(8,128)(2,1)} fusion(bf16[512,768]{1,0:T(8,128)(2,1)} %get-tuple-element.107, bf16[512,3072]{1,0:T(8,128)(2,1)} %get-tuple-element.153), kind=kOutput, calls=%fused_computation.6 | convolution fusion | flops 604569600 | bytes 2752512 | tf_op jit(solution)/shard_map/dot_general | solution.py:30
  142.9 3.6 %all-to-all-start.4 = ((bf16[8,64,768]{2,1,0:T(8,128)(2,1)}), bf16[8,64,768]{2,1,0:T(8,128)(2,1)S(1)}, u32[]{:S(2)}, u32[]{:S(2)}) async-start(bf16[8,64,768]{2,1,0:T(8,128)(2,1)} %bitcast.40), calls=%async_computation.4 | async-start | bytes 1572864 | tf_op jit(solution)/shard_map/all_to_all | solution.py:711
  146.6 3.1 %convolution_convert_fusion.1 = bf16[768,768]{1,0:T(8,128)(2,1)} fusion(bf16[512,768]{1,0:T(8,128)(2,1)S(1)} %bitcast.160, bf16[512,3072]{1,0:T(8,128)(2,1)} %get-tuple-element.150), kind=kOutput, calls=%fused_computation.7 | convolution fusion | flops 604569600 | bytes 2752512 | tf_op jit(solution)/shard_map/dot_general | solution.py:30
  155.0 3.1 %add_convert_fusion = bf16[768,768]{1,0:T(8,128)(2,1)} fusion(bf16[768,768]{1,0:T(8,128)(2,1)} %collective-permute-done.8, bf16[512,768]{1,0:T(8,128)(2,1)S(1)} %copy-done.16, bf16[512,3072]{1,0:T(8,128)(2,1)S(1)} %copy-done.23), kind=kOutput, calls=%fused_computation.2 | convolution fusion | flops 605749248 | bytes 3932160 | tf_op jit(solution)/shard_map/dot_general | solution.py:30
  158.5 9.1 %all-to-all-done.4 = bf16[8,64,768]{2,1,0:T(8,128)(2,1)S(1)} async-done(((bf16[8,64,768]{2,1,0:T(8,128)(2,1)}), bf16[8,64,768]{2,1,0:T(8,128)(2,1)S(1)}, u32[]{:S(2)}, u32[]{:S(2)}) %all-to-all-start.4) | async-done | bytes 786464 | tf_op jit(solution)/shard_map/all_to_all | solution.py:711
  168.4 3.4 %mlp_back.1 = (f32[128,768]{1,0:T(8,128)}, bf16[128,768]{1,0:T(8,128)(2,1)}, f32[1,768]{1,0:T(1,128)}, bf16[4,192,128]{2,1,0:T(8,128)(2,1)}) custom-call(bf16[512,768]{1,0:T(8,128)(2,1)} %bitcast.176, bf16[512,128]{1,0:T(8,128)(2,1)} %get-tuple-element.208.disp_ref, f32[128,768]{1,0:T(8,128)} %get-tuple-element.101.resid_ref, f32[128,768]{1,0:T(8,128)} %bitcast.181, ...), custom_call_target="tpu_custom_call" | custom-call | bytes 13600000 | tf_op jit(solution)/shard_map/mlp_back/pallas_call | solution.py:524
  171.7 3.4 %all-to-all-start.5 = ((bf16[4,192,128]{2,1,0:T(8,128)(2,1)}), bf16[4,192,128]{2,1,0:T(8,128)(2,1)S(1)}, u32[]{:S(2)}, u32[]{:S(2)}) async-start(bf16[4,192,128]{2,1,0:T(8,128)(2,1)} %get-tuple-element.110), calls=%async_computation.5 | async-start | bytes 393216 | tf_op jit(solution)/shard_map/all_to_all | solution.py:711
  178.1 3.2 %side_grad.1 = f32[8,96,896]{2,1,0:T(8,128)} custom-call(bf16[4,192,128]{2,1,0:T(8,128)(2,1)} %copy-done.10, bf16[128,768]{1,0:T(8,128)(2,1)} %get-tuple-element.112.grad_ref, f32[768,128]{1,0:T(8,128)} %get-tuple-element.113.router_ref), custom_call_target="tpu_custom_call" | custom-call | bytes 170000 | tf_op jit(solution)/shard_map/side_grad/pallas_call | solution.py:611
  182.6 4.6 %all-to-all-start.6 = ((bf16[8,64,768]{2,1,0:T(8,128)(2,1)}), bf16[8,64,768]{2,1,0:T(8,128)(2,1)S(1)}, u32[]{:S(2)}, u32[]{:S(2)}) async-start(bf16[8,64,768]{2,1,0:T(8,128)(2,1)} %bitcast.47), calls=%async_computation.6 | async-start | bytes 1572864 | tf_op jit(solution)/shard_map/all_to_all | solution.py:711
  189.8 9.4 %attention_backward.2 = (f32[4,128,192]{2,1,0:T(8,128)}, bf16[1,4,128,384]{3,2,1,0:T(8,128)(2,1)}, f32[1,3,5,256]{3,2,1,0:T(8,128)}) custom-call(s32[4]{0:T(128)} %get-tuple-element.211.place_ref, bf16[4,128,192]{2,1,0:T(8,128)(2,1)} %get-tuple-element.91.q_ref, bf16[1,4,128,384]{3,2,1,0:T(8,128)(2,1)} %bitcast.183, s32[4,128,1]{2,1,0:T(8,128)} %copy.55.refs_2_.start_ref, ...), custom_call_target="tpu_custom_call" | custom-call | bytes 27200000 | tf_op jit(solution)/shard_map/attention_backward/pallas_call | solution.py:313
  204.1 9.5 %attention_backward.3 = (f32[4,128,192]{2,1,0:T(8,128)}, f32[1,4,128,384]{3,2,1,0:T(8,128)}, f32[1,3,5,256]{3,2,1,0:T(8,128)}) custom-call(s32[4]{0:T(128)} %get-tuple-element.210.place_ref, bf16[4,128,192]{2,1,0:T(8,128)(2,1)} %get-tuple-element.91.q_ref, bf16[1,4,128,384]{3,2,1,0:T(8,128)(2,1)} %bitcast.182, s32[4,128,1]{2,1,0:T(8,128)} %copy.55.refs_2_.start_ref, ...), custom_call_target="tpu_custom_call" | custom-call | bytes 3400000 | tf_op jit(solution)/shard_map/attention_backward/pallas_call | solution.py:313
  213.6 3.8 %collective-permute-done.11 = bf16[768,768]{1,0:T(8,128)(2,1)} collective-permute-done((bf16[768,768]{1,0:T(8,128)(2,1)}, bf16[768,768]{1,0:T(8,128)(2,1)}, u32[]{:S(2)}, u32[]{:S(2)}) %collective-permute-start.11) | collective-permute-done | bytes 1179680 | tf_op jit(solution)/shard_map/ppermute | solution.py:694
  219.3 4.5 %project_back.1 = (bf16[512,576]{1,0:T(8,128)(2,1)}, f32[1,768]{1,0:T(1,128)}, bf16[4,128,768]{2,1,0:T(8,128)(2,1)}) custom-call(f32[4,128,192]{2,1,0:T(8,128)} %get-tuple-element.127.dq_ref, f32[4,128,192]{2,1,0:T(8,128)} %get-tuple-element.128.dq_other_ref, f32[4,128,384]{2,1,0:T(8,128)} %bitcast.186, bf16[4,128,384]{2,1,0:T(8,128)(2,1)} %copy-done.19, ...), custom_call_target="tpu_custom_call" | custom-call | bytes 13600000 | tf_op jit(solution)/shard_map/project_back/pallas_call | solution.py:566
  223.8 3.4 %qkv_grad.1 = f32[8,96,576]{2,1,0:T(8,128)} custom-call(bf16[4,128,768]{2,1,0:T(8,128)(2,1)} %get-tuple-element.126.h_ref, bf16[512,576]{1,0:T(8,128)(2,1)} %get-tuple-element.131.dproj_ref), custom_call_target="tpu_custom_call" | custom-call | bytes 170000 | tf_op jit(solution)/shard_map/qkv_grad/pallas_call | solution.py:589
  229.4 5.1 %all-to-all-start.7 = ((bf16[4,128,768]{2,1,0:T(8,128)(2,1)}), bf16[4,128,768]{2,1,0:T(8,128)(2,1)S(1)}, u32[]{:S(2)}, u32[]{:S(2)}) async-start(bf16[4,128,768]{2,1,0:T(8,128)(2,1)} %get-tuple-element.143), calls=%async_computation.7 | async-start | bytes 1572864 | tf_op jit(solution)/shard_map/all_to_all | solution.py:711
  244.2 5.7 %collective-permute-done.15 = bf16[8,24,576]{2,1,0:T(8,128)(2,1)S(1)} collective-permute-done((bf16[8,24,576]{2,1,0:T(8,128)(2,1)S(1)}, bf16[8,24,576]{2,1,0:T(8,128)(2,1)S(1)}, u32[]{:S(2)}, u32[]{:S(2)}) %collective-permute-start.15) | collective-permute-done | bytes 221216 | tf_op jit(solution)/shard_map/ppermute | solution.py:694
  252.7 3.4 %add_bitcast_fusion = f32[1,768,768]{2,1,0:T(8,128)} fusion(bf16[768,768]{1,0:T(8,128)(2,1)} %collective-permute-done.9, f32[768,768]{1,0:T(8,128)S(1)} %fusion.3, bf16[768,768]{1,0:T(8,128)(2,1)} %collective-permute-done.16), kind=kLoop, calls=%fused_computation | loop fusion | flops 2359296 | bytes 7077888 | tf_op jit(solution)/shard_map/broadcast_in_dim | solution.py:984
  256.2 3.3 %fusion.5 = f32[768,768]{1,0:T(8,128)} fusion(bf16[512,768]{1,0:T(8,128)(2,1)S(1)} %bitcast.163, bf16[512,3072]{1,0:T(8,128)(2,1)} %get-tuple-element.150), kind=kOutput, calls=%fused_computation.26 | convolution fusion | flops 603979776 | bytes 3932160 | tf_op jit(solution)/shard_map/dot_general | solution.py:30
  266.3 4.0 %add_bitcast_fusion.1 = f32[1,768,768]{2,1,0:T(8,128)} fusion(bf16[768,768]{1,0:T(8,128)(2,1)} %collective-permute-done.11, f32[768,768]{1,0:T(8,128)} %fusion.5, bf16[768,768]{1,0:T(8,128)(2,1)} %collective-permute-done.17), kind=kLoop, calls=%fused_computation.1 | loop fusion | flops 2359296 | bytes 7077888 | tf_op jit(solution)/shard_map/broadcast_in_dim | solution.py:983
  274.9 3.6 %collective-permute-done.23 = bf16[24,3456]{1,0:T(8,128)(2,1)S(1)} collective-permute-done((bf16[24,3456]{1,0:T(8,128)(2,1)}, bf16[24,3456]{1,0:T(8,128)(2,1)S(1)}, u32[]{:S(2)}, u32[]{:S(2)}) %collective-permute-start.23) | collective-permute-done | bytes 165920 | tf_op jit(solution)/shard_map/ppermute | solution.py:694
  (219 shorter events, 92.1 us)
Async XLA Ops:
  3.0 20.8 %collective-permute-start = (bf16[128,768]{1,0:T(8,128)(2,1)S(1)}, bf16[128,768]{1,0:T(8,128)(2,1)S(1)}, u32[]{:S(2)}, u32[]{:S(2)}) collective-permute-start(bf16[128,768]{1,0:T(8,128)(2,1)S(1)} %multiply_convert_fusion.h0_ref), channel_id=1, source_target_pairs={{0,2},{2,4},{4,6},{6,0},{1,3},{3,5},{5,7},{7,1},{8,10},{10,12},{12... | collective-permute-start | bytes 589832 | tf_op jit(solution)/shard_map/ppermute | solution.py:702
  6.1 17.7 %collective-permute-start.1 = (bf16[128,768]{1,0:T(8,128)(2,1)S(1)}, bf16[128,768]{1,0:T(8,128)(2,1)S(1)}, u32[]{:S(2)}, u32[]{:S(2)}) collective-permute-start(bf16[128,768]{1,0:T(8,128)(2,1)S(1)} %multiply_convert_fusion.h0_ref), channel_id=1, source_target_pairs={{0,4},{2,6},{4,0},{6,2},{1,5},{3,7},{5,1},{7,3},{8,12},{10,14},{12... | collective-permute-start | bytes 589832 | tf_op jit(solution)/shard_map/ppermute | solution.py:702
  8.7 15.1 %collective-permute-start.2 = (bf16[128,768]{1,0:T(8,128)(2,1)S(1)}, bf16[128,768]{1,0:T(8,128)(2,1)S(1)}, u32[]{:S(2)}, u32[]{:S(2)}) collective-permute-start(bf16[128,768]{1,0:T(8,128)(2,1)S(1)} %multiply_convert_fusion.h0_ref), channel_id=1, source_target_pairs={{0,6},{2,0},{4,2},{6,4},{1,7},{3,1},{5,3},{7,5},{8,14},{10,8},{12,... | collective-permute-start | bytes 589832 | tf_op jit(solution)/shard_map/ppermute | solution.py:702
  12.2 24.1 %all-to-all-start = ((bf16[8,48,576]{2,1,0:T(8,128)(2,1)}), bf16[8,48,576]{2,1,0:T(8,128)(2,1)S(1)}, u32[]{:S(2)}, u32[]{:S(2)}) async-start(bf16[8,48,576]{2,1,0:T(8,128)(2,1)} %reshape.160), calls=%async_computation | async-start | bytes 983040 | tf_op jit(solution)/shard_map/all_to_all | solution.py:711
  36.3 37.1 %all-to-all-start.1 = ((bf16[8,88,896]{2,1,0:T(8,128)(2,1)}), bf16[8,88,896]{2,1,0:T(8,128)(2,1)S(1)}, u32[]{:S(2)}, u32[]{:S(2)}) async-start(bf16[8,88,896]{2,1,0:T(8,128)(2,1)} %pad_maximum_fusion), calls=%async_computation.1 | async-start | bytes 2523136 | tf_op jit(solution)/shard_map/all_to_all | solution.py:711
  40.1 1.9 collective-permute-start.3
  46.8 18.6 %collective-permute-start.4 = (bf16[4,128,384]{2,1,0:T(8,128)(2,1)}, bf16[4,128,384]{2,1,0:T(8,128)(2,1)S(1)}, u32[]{:S(2)}, u32[]{:S(2)}) collective-permute-start(bf16[4,128,384]{2,1,0:T(8,128)(2,1)} %get-tuple-element.92.refs_0_), channel_id=1, source_target_pairs={{0,1},{1,0},{2,3},{3,2},{4,5},{5,4},{6,7},{7,6},{8,9},{9,8},{10,11... | collective-permute-start | bytes 1179656 | tf_op jit(solution)/shard_map/ppermute | solution.py:694
  73.4 10.0 %collective-permute-start.5 = (bf16[8,24,896]{2,1,0:T(8,128)(2,1)S(1)}, bf16[8,24,896]{2,1,0:T(8,128)(2,1)S(1)}, u32[]{:S(2)}, u32[]{:S(2)}) collective-permute-start(bf16[8,24,896]{2,1,0:T(8,128)(2,1)S(1)} %get-tuple-element.197), channel_id=1, source_target_pairs={{0,16},{16,0},{1,17},{17,1},{2,18},{18,2},{3,19},{19,3},{4,20},{20... | collective-permute-start | bytes 1032200 | tf_op jit(solution)/shard_map/ppermute | solution.py:694
  75.0 13.6 %all-to-all-start.2 = ((bf16[4,192,128]{2,1,0:T(8,128)(2,1)}), bf16[4,192,128]{2,1,0:T(8,128)(2,1)S(1)}, u32[]{:S(2)}, u32[]{:S(2)}) async-start(bf16[4,192,128]{2,1,0:T(8,128)(2,1)} %get-tuple-element.97), calls=%async_computation.2 | async-start | bytes 393216 | tf_op jit(solution)/shard_map/all_to_all | solution.py:711
  88.6 2.1 collective-permute-start.6
  95.3 24.2 %all-to-all-start.3 = ((bf16[8,64,768]{2,1,0:T(8,128)(2,1)}), bf16[8,64,768]{2,1,0:T(8,128)(2,1)S(1)}, u32[]{:S(2)}, u32[]{:S(2)}) async-start(bf16[8,64,768]{2,1,0:T(8,128)(2,1)} %bitcast.185), calls=%async_computation.3 | async-start | bytes 1572864 | tf_op jit(solution)/shard_map/all_to_all | solution.py:711
  142.9 12.1 %collective-permute-start.8 = (bf16[768,768]{1,0:T(8,128)(2,1)}, bf16[768,768]{1,0:T(8,128)(2,1)}, u32[]{:S(2)}, u32[]{:S(2)}) collective-permute-start(bf16[768,768]{1,0:T(8,128)(2,1)} %convolution_convert_fusion), channel_id=1, source_target_pairs={{0,8},{8,0},{1,9},{9,1},{2,10},{10,2},{3,11},{11,3},{4,12},{12,4},... | collective-permute-start | bytes 3538952 | tf_op jit(solution)/shard_map/ppermute | solution.py:694
  142.9 24.6 %all-to-all-start.4 = ((bf16[8,64,768]{2,1,0:T(8,128)(2,1)}), bf16[8,64,768]{2,1,0:T(8,128)(2,1)S(1)}, u32[]{:S(2)}, u32[]{:S(2)}) async-start(bf16[8,64,768]{2,1,0:T(8,128)(2,1)} %bitcast.40), calls=%async_computation.4 | async-start | bytes 1572864 | tf_op jit(solution)/shard_map/all_to_all | solution.py:711
  149.7 25.4 %collective-permute-start.7 = (bf16[768,768]{1,0:T(8,128)(2,1)}, bf16[768,768]{1,0:T(8,128)(2,1)S(1)}, u32[]{:S(2)}, u32[]{:S(2)}) collective-permute-start(bf16[768,768]{1,0:T(8,128)(2,1)} %convolution_convert_fusion.1), channel_id=1, source_target_pairs={{0,8},{8,0},{1,9},{9,1},{2,10},{10,2},{3,11},{11,3},{4,12},{12,4},... | collective-permute-start | bytes 3538952 | tf_op jit(solution)/shard_map/ppermute | solution.py:694
  158.1 42.8 %collective-permute-start.9 = (bf16[768,768]{1,0:T(8,128)(2,1)}, bf16[768,768]{1,0:T(8,128)(2,1)}, u32[]{:S(2)}, u32[]{:S(2)}) collective-permute-start(bf16[768,768]{1,0:T(8,128)(2,1)} %add_convert_fusion), channel_id=1, source_target_pairs={{0,16},{16,0},{1,17},{17,1},{2,18},{18,2},{3,19},{19,3},{4,20},{20... | collective-permute-start | bytes 3538952 | tf_op jit(solution)/shard_map/ppermute | solution.py:694
  171.7 10.8 %all-to-all-start.5 = ((bf16[4,192,128]{2,1,0:T(8,128)(2,1)}), bf16[4,192,128]{2,1,0:T(8,128)(2,1)S(1)}, u32[]{:S(2)}, u32[]{:S(2)}) async-start(bf16[4,192,128]{2,1,0:T(8,128)(2,1)} %get-tuple-element.110), calls=%async_computation.5 | async-start | bytes 393216 | tf_op jit(solution)/shard_map/all_to_all | solution.py:711
  182.6 34.8 %all-to-all-start.6 = ((bf16[8,64,768]{2,1,0:T(8,128)(2,1)}), bf16[8,64,768]{2,1,0:T(8,128)(2,1)S(1)}, u32[]{:S(2)}, u32[]{:S(2)}) async-start(bf16[8,64,768]{2,1,0:T(8,128)(2,1)} %bitcast.47), calls=%async_computation.6 | async-start | bytes 1572864 | tf_op jit(solution)/shard_map/all_to_all | solution.py:711
  188.6 10.5 %collective-permute-start.10 = (bf16[8,48,896]{2,1,0:T(8,128)(2,1)S(1)}, bf16[8,48,896]{2,1,0:T(8,128)(2,1)}, u32[]{:S(2)}, u32[]{:S(2)}) collective-permute-start(bf16[8,48,896]{2,1,0:T(8,128)(2,1)S(1)} %fusion.19), channel_id=1, source_target_pairs={{0,8},{8,0},{1,9},{9,1},{2,10},{10,2},{3,11},{11,3},{4,12},{12,4},... | collective-permute-start | bytes 2064392 | tf_op jit(solution)/shard_map/ppermute | solution.py:694
  188.7 28.7 %collective-permute-start.11 = (bf16[768,768]{1,0:T(8,128)(2,1)}, bf16[768,768]{1,0:T(8,128)(2,1)}, u32[]{:S(2)}, u32[]{:S(2)}) collective-permute-start(bf16[768,768]{1,0:T(8,128)(2,1)} %add_convert_fusion.1), channel_id=1, source_target_pairs={{0,16},{16,0},{1,17},{17,1},{2,18},{18,2},{3,19},{19,3},{4,20},{20... | collective-permute-start | bytes 3538952 | tf_op jit(solution)/shard_map/ppermute | solution.py:694
  200.9 17.7 %collective-permute-start.13 = (bf16[4,128,384]{2,1,0:T(8,128)(2,1)}, bf16[4,128,384]{2,1,0:T(8,128)(2,1)S(1)}, u32[]{:S(2)}, u32[]{:S(2)}) collective-permute-start(bf16[4,128,384]{2,1,0:T(8,128)(2,1)} %bitcast.53), channel_id=1, source_target_pairs={{0,1},{1,0},{2,3},{3,2},{4,5},{5,4},{6,7},{7,6},{8,9},{9,8},{10,11... | collective-permute-start | bytes 1179656 | tf_op jit(solution)/shard_map/ppermute | solution.py:694
  203.6 46.5 %collective-permute-start.16 = (bf16[768,768]{1,0:T(8,128)(2,1)}, bf16[768,768]{1,0:T(8,128)(2,1)}, u32[]{:S(2)}, u32[]{:S(2)}) collective-permute-start(bf16[768,768]{1,0:T(8,128)(2,1)} %convolution_convert_fusion.3), channel_id=1, source_target_pairs={{0,8},{8,0},{1,9},{9,1},{2,10},{10,2},{3,11},{11,3},{4,12},{12,4},... | collective-permute-start | bytes 3538952 | tf_op jit(solution)/shard_map/ppermute | solution.py:694
  203.6 46.5 %collective-permute-start.17 = (bf16[768,768]{1,0:T(8,128)(2,1)}, bf16[768,768]{1,0:T(8,128)(2,1)}, u32[]{:S(2)}, u32[]{:S(2)}) collective-permute-start(bf16[768,768]{1,0:T(8,128)(2,1)} %convolution_convert_fusion.2), channel_id=1, source_target_pairs={{0,8},{8,0},{1,9},{9,1},{2,10},{10,2},{3,11},{11,3},{4,12},{12,4},... | collective-permute-start | bytes 3538952 | tf_op jit(solution)/shard_map/ppermute | solution.py:694
  218.2 18.6 %collective-permute-start.12 = (bf16[8,24,896]{2,1,0:T(8,128)(2,1)}, bf16[8,24,896]{2,1,0:T(8,128)(2,1)}, u32[]{:S(2)}, u32[]{:S(2)}) collective-permute-start(bf16[8,24,896]{2,1,0:T(8,128)(2,1)} %fusion.22), channel_id=1, source_target_pairs={{0,16},{16,0},{1,17},{17,1},{2,18},{18,2},{3,19},{19,3},{4,20},{20... | collective-permute-start | bytes 1032200 | tf_op jit(solution)/shard_map/ppermute | solution.py:694
  229.4 9.4 %collective-permute-start.14 = (bf16[8,48,576]{2,1,0:T(8,128)(2,1)}, bf16[8,48,576]{2,1,0:T(8,128)(2,1)}, u32[]{:S(2)}, u32[]{:S(2)}) collective-permute-start(bf16[8,48,576]{2,1,0:T(8,128)(2,1)} %fusion.21), channel_id=1, source_target_pairs={{0,8},{8,0},{1,9},{9,1},{2,10},{10,2},{3,11},{11,3},{4,12},{12,4},... | collective-permute-start | bytes 1327112 | tf_op jit(solution)/shard_map/ppermute | solution.py:694
  229.4 31.0 %all-to-all-start.7 = ((bf16[4,128,768]{2,1,0:T(8,128)(2,1)}), bf16[4,128,768]{2,1,0:T(8,128)(2,1)S(1)}, u32[]{:S(2)}, u32[]{:S(2)}) async-start(bf16[4,128,768]{2,1,0:T(8,128)(2,1)} %get-tuple-element.143), calls=%async_computation.7 | async-start | bytes 1572864 | tf_op jit(solution)/shard_map/all_to_all | solution.py:711
  240.4 3.8 %collective-permute-start.19 = (f32[24,128]{1,0:T(8,128)S(1)}, f32[24,128]{1,0:T(8,128)S(1)}, u32[]{:S(2)}, u32[]{:S(2)}) collective-permute-start(f32[24,128]{1,0:T(8,128)S(1)} %pad.28), channel_id=1, source_target_pairs={{0,1},{1,0},{2,3},{3,2},{4,5},{5,4},{6,7},{7,6},{8,9},{9,8},{10,11... | collective-permute-start | bytes 36872 | tf_op jit(solution)/shard_map/ppermute | solution.py:694
  242.0 7.9 %collective-permute-start.15 = (bf16[8,24,576]{2,1,0:T(8,128)(2,1)S(1)}, bf16[8,24,576]{2,1,0:T(8,128)(2,1)S(1)}, u32[]{:S(2)}, u32[]{:S(2)}) collective-permute-start(bf16[8,24,576]{2,1,0:T(8,128)(2,1)S(1)} %fusion.27), channel_id=1, source_target_pairs={{0,16},{16,0},{1,17},{17,1},{2,18},{18,2},{3,19},{19,3},{4,20},{20... | collective-permute-start | bytes 663560 | tf_op jit(solution)/shard_map/ppermute | solution.py:694
  252.1 8.1 %collective-permute-start.18 = (bf16[4,24,1472]{2,1,0:T(8,128)(2,1)S(1)}, bf16[4,24,1472]{2,1,0:T(8,128)(2,1)S(1)}, u32[]{:S(2)}, u32[]{:S(2)}) collective-permute-start(bf16[4,24,1472]{2,1,0:T(8,128)(2,1)S(1)} %fusion.23), channel_id=1, source_target_pairs={{0,1},{1,0},{2,3},{3,2},{4,5},{5,4},{6,7},{7,6},{8,9},{9,8},{10,11... | collective-permute-start | bytes 847880 | tf_op jit(solution)/shard_map/ppermute | solution.py:694
  261.0 9.3 %collective-permute-start.20 = (bf16[24,1728]{1,0:T(8,128)(2,1)S(1)}, bf16[24,1728]{1,0:T(8,128)(2,1)S(1)}, u32[]{:S(2)}, u32[]{:S(2)}) collective-permute-start(bf16[24,1728]{1,0:T(8,128)(2,1)S(1)} %get-tuple-element.200), channel_id=1, source_target_pairs={{0,2},{2,4},{4,6},{6,0},{1,3},{3,5},{5,7},{7,1},{8,10},{10,12},{12... | collective-permute-start | bytes 248840 | tf_op jit(solution)/shard_map/ppermute | solution.py:702
  262.5 7.9 %collective-permute-start.21 = (bf16[24,1728]{1,0:T(8,128)(2,1)S(1)}, bf16[24,1728]{1,0:T(8,128)(2,1)S(1)}, u32[]{:S(2)}, u32[]{:S(2)}) collective-permute-start(bf16[24,1728]{1,0:T(8,128)(2,1)S(1)} %get-tuple-element.199), channel_id=1, source_target_pairs={{0,4},{2,6},{4,0},{6,2},{1,5},{3,7},{5,1},{7,3},{8,12},{10,14},{12... | collective-permute-start | bytes 248840 | tf_op jit(solution)/shard_map/ppermute | solution.py:702
  264.8 5.6 %collective-permute-start.22 = (bf16[24,1728]{1,0:T(8,128)(2,1)S(1)}, bf16[24,1728]{1,0:T(8,128)(2,1)S(1)}, u32[]{:S(2)}, u32[]{:S(2)}) collective-permute-start(bf16[24,1728]{1,0:T(8,128)(2,1)S(1)} %get-tuple-element.198), channel_id=1, source_target_pairs={{0,6},{2,0},{4,2},{6,4},{1,7},{3,1},{5,3},{7,5},{8,14},{10,8},{12,... | collective-permute-start | bytes 248840 | tf_op jit(solution)/shard_map/ppermute | solution.py:702
  272.9 5.6 %collective-permute-start.23 = (bf16[24,3456]{1,0:T(8,128)(2,1)}, bf16[24,3456]{1,0:T(8,128)(2,1)S(1)}, u32[]{:S(2)}, u32[]{:S(2)}) collective-permute-start(bf16[24,3456]{1,0:T(8,128)(2,1)} %assemble.1), channel_id=1, source_target_pairs={{0,16},{16,0},{1,17},{17,1},{2,18},{18,2},{3,19},{19,3},{4,20},{20... | collective-permute-start | bytes 497672 | tf_op jit(solution)/shard_map/ppermute | solution.py:694
  (41 other events, 255.7 us)

commit v2 on v1

--- a/solution.py
+++ b/solution.py
@@ -651,8 +651,8 @@
     )(own, *parts)
 
 
-def unpack_kernel(own_ref, pair_ref, came_ref, attn_ref, router_ref, qkv_ref, small_ref):
-    experts = router_ref.shape[2]
+def unpack_kernel(own_ref, pair_ref, came_ref, attn_ref, router_ref, qkv_ref, small_ref, *scratch):
+    experts = router_ref.shape[0] if scratch else router_ref.shape[-1]
     last = 4 * D + 128
     width = small_ref.shape[1]
     small = jnp.zeros(small_ref.shape, F32)
@@ -660,25 +660,38 @@
         for part in range(2):
             value = ref[part].astype(F32)
             attn_ref[near * 2 + part] = value[:, :D]
-            router_ref[near * 2 + part] = value[:, D : D + experts]
+            if scratch:
+                scratch[0][near * 2 + part] = value[:, D : D + 128]
+            else:
+                router_ref[near * 2 + part] = value[:, D : D + experts]
             qkv_ref[near * 2 + part] = value[:, D + 128 : last]
             small = small + (value[:, last : last + width] + value[:, last + width :])
     small_ref[...] = small
+    if scratch:
+        count, lanes = router_ref.shape
+        wide = scratch[0][...].reshape(lanes, 128)
+        wide = jnp.concatenate((wide, jnp.zeros((-lanes % 128, 128), F32)), axis=0)
+        router_ref[...] = wide.T[:count, :lanes]
 
 
 def unpack(own, pair, came, experts):
     rows = pair.shape[1]
     width = (pair.shape[2] - 4 * D - 128) // 2
+    flip = rows % 8 == 0 and 4 * rows <= 128
+    router_shape = (experts, 4 * rows) if flip else (4, rows, experts)
+    shapes = [(4, rows, D), router_shape, (4, rows, 3 * D), (rows, width)]
     outs = pl.pallas_call(
         unpack_kernel,
         in_specs=[SM] + [VM] * 2,
         out_specs=[VM] * 4,
-        out_shape=[jax.ShapeDtypeStruct((4, rows, n), F32) for n in (D, experts, 3 * D)]
-        + [jax.ShapeDtypeStruct((rows, width), F32)],
+        out_shape=[jax.ShapeDtypeStruct(shape, F32) for shape in shapes],
+        scratch_shapes=[pltpu.VMEM((4, rows, 128), F32)] if flip else [],
         cost_estimate=cost(0.05),
         name="unpack",
     )(own.astype(jnp.int32), pair, came)
-    return [out.reshape(4 * rows, -1) for out in outs[:3]] + [outs[3]]
+    attn, router, qkv, small = outs
+    router = router.T if flip else router.reshape(4 * rows, experts)
+    return attn.reshape(4 * rows, -1), router, qkv.reshape(4 * rows, -1), small
 
 
 def gelu_parts(hidden):

time: 289 us -> 287 us (level)
    unnamed x82 -> x81, local copies, waits for them, and re-layouts: 6.33 us -> 4.87 us
where the time goes in v2:
time: 287 us; the launch traced here: 286 us
  waiting for transfers between devices  81.5 us (28%)
  Pallas kernels  73.6 us (26%)
  starting transfers between devices  59.8 us (21%)
  matrix products  26.5 us (9%)
  local copies, waits for them, and re-layouts  23.3 us (8%)
  other arithmetic  19.8 us (7%)
    all_to_all x8, waiting for transfers between devices, exchange(): return lax.all_to_all(value, axes, split_axis=0, concat_axis=0, tiled=True)  45.9 us
    ppermute x19, waiting for transfers between devices, swap(): return lax.ppermute(value, axis, [(0, 1), (1, 0)])  35.6 us
    all_to_all x8, starting transfers between devices, exchange(): return lax.all_to_all(value, axes, split_axis=0, concat_axis=0, tiled=True)  34 us
    dot_general x9, matrix products, dotf(): return lax.dot_general(a, b, dims, preferred_element_type=F32)  25 us
    pallas_call x1, Pallas kernels, expert_layer(): pl.pallas_call(expert_kernel, grid_spec=pltpu.PrefetchScalarGridSpec(num_...  19.2 us
    pallas_call x2, Pallas kernels, attention_backward(): pl.pallas_call(backward_kernel, in_specs=[SM] + [VM] * 7, out_specs=[VM]...  18.9 us
    ppermute x19, starting transfers between devices, swap(): return lax.ppermute(value, axis, [(0, 1), (1, 0)])  13.5 us
    ppermute x6, starting transfers between devices, turn(): lax.ppermute(value, 'g', [(j, (j + step) % GROUPS) for j in range(GROUPS)])  12.3 us
  transfers between devices with their start and end apart: 33, of which 15 were waited for; matrix products, arithmetic and copies ran while one was open for 19% of the time, Pallas kernels for 16%

profile of v2, /device:TPU:0, one launch (start us, length us, event | category | flops | bytes accessed | tf_op | source)
XLA Modules:
  0.0 285.9 jit_solution(6201385963369575006)
XLA Ops:
  12.2 3.5 %all-to-all-start = ((bf16[8,48,576]{2,1,0:T(8,128)(2,1)}), bf16[8,48,576]{2,1,0:T(8,128)(2,1)S(1)}, u32[]{:S(2)}, u32[]{:S(2)}) async-start(bf16[8,48,576]{2,1,0:T(8,128)(2,1)} %reshape.157), calls=%async_computation | async-start | bytes 983040 | tf_op jit(solution)/shard_map/all_to_all | solution.py:724
  23.8 12.5 %all-to-all-done = bf16[8,48,576]{2,1,0:T(8,128)(2,1)S(1)} async-done(((bf16[8,48,576]{2,1,0:T(8,128)(2,1)}), bf16[8,48,576]{2,1,0:T(8,128)(2,1)S(1)}, u32[]{:S(2)}, u32[]{:S(2)}) %all-to-all-start) | async-done | bytes 442400 | tf_op jit(solution)/shard_map/all_to_all | solution.py:724
  36.3 3.8 %all-to-all-start.1 = ((bf16[8,88,896]{2,1,0:T(8,128)(2,1)}), bf16[8,88,896]{2,1,0:T(8,128)(2,1)S(1)}, u32[]{:S(2)}, u32[]{:S(2)}) async-start(bf16[8,88,896]{2,1,0:T(8,128)(2,1)} %pad_maximum_fusion), calls=%async_computation.1 | async-start | bytes 2523136 | tf_op jit(solution)/shard_map/all_to_all | solution.py:724
  43.3 3.5 %project.1 = (bf16[4,128,192]{2,1,0:T(8,128)(2,1)}, bf16[4,128,384]{2,1,0:T(8,128)(2,1)}, bf16[4,128,768]{2,1,0:T(8,128)(2,1)}) custom-call(s32[1]{0:T(128)} %bitcast.2.own_ref, bf16[128,768]{1,0:T(8,128)(2,1)} %copy-done.15, bf16[128,768]{1,0:T(8,128)(2,1)} %copy-done.24, bf16[128,768]{1,0:T(8,128)(2,1)} %copy-done.25, bf16[128,768]{1,0:T(8,128)(2,1)} %copy-done.26, ...), custom_call_target="tpu_custom_call" | custom-call | bytes 170000 | tf_op jit(solution)/shard_map/project/pallas_call | solution.py:345
  50.2 15.2 %collective-permute-done.4.refs_1_ = bf16[4,128,384]{2,1,0:T(8,128)(2,1)S(1)} collective-permute-done((bf16[4,128,384]{2,1,0:T(8,128)(2,1)}, bf16[4,128,384]{2,1,0:T(8,128)(2,1)S(1)}, u32[]{:S(2)}, u32[]{:S(2)}) %collective-permute-start.4) | collective-permute-done | bytes 393248 | tf_op jit(solution)/shard_map/ppermute | solution.py:707
  66.1 7.2 %attention_forward.1 = (bf16[4,192,128]{2,1,0:T(8,128)(2,1)}, f32[4,128,192]{2,1,0:T(8,128)}, f32[4,384,128]{2,1,0:T(8,128)}) custom-call(s32[5]{0:T(128)} %concatenate.44.place_ref, bf16[4,128,192]{2,1,0:T(8,128)(2,1)} %get-tuple-element.91.q_ref, bf16[4,128,384]{2,1,0:T(8,128)(2,1)} %get-tuple-element.92.refs_0_, bf16[4,128,384]{2,1,0:T(8,128)(2,1)} %copy-done.13, ...), custom_call_target="tpu_custom_call" | custom-call | bytes 23800000 | tf_op jit(solution)/shard_map/attention_forward/pallas_call | solution.py:201
  75.0 6.3 %all-to-all-start.2 = ((bf16[4,192,128]{2,1,0:T(8,128)(2,1)}), bf16[4,192,128]{2,1,0:T(8,128)(2,1)S(1)}, u32[]{:S(2)}, u32[]{:S(2)}) async-start(bf16[4,192,128]{2,1,0:T(8,128)(2,1)} %get-tuple-element.97), calls=%async_computation.2 | async-start | bytes 393216 | tf_op jit(solution)/shard_map/all_to_all | solution.py:724
  83.6 5.0 %all-to-all-done.2.att_ref = bf16[4,192,128]{2,1,0:T(8,128)(2,1)S(1)} async-done(((bf16[4,192,128]{2,1,0:T(8,128)(2,1)}), bf16[4,192,128]{2,1,0:T(8,128)(2,1)S(1)}, u32[]{:S(2)}, u32[]{:S(2)}) %all-to-all-start.2) | async-done | bytes 196640 | tf_op jit(solution)/shard_map/all_to_all | solution.py:724
  92.0 3.3 %mlp_in.1 = (f32[128,768]{1,0:T(8,128)}, bf16[512,768]{1,0:T(8,128)(2,1)}) custom-call(bf16[4,192,128]{2,1,0:T(8,128)(2,1)} %copy-done.10, bf16[4,192,768]{2,1,0:T(8,128)(2,1)} %bitcast.152, f32[128,768]{1,0:T(8,128)} %bitcast.154, f32[1,768]{1,0:T(1,128)} %broadcast_in_dim.37.gain_ref, bf16[512,128]{1,0:T(8,128)(2,1)} %get-tuple-element.168.disp_ref), custom_call_target="tpu_custom_call" | custom-call | bytes 170000 | tf_op jit(solution)/shard_map/mlp_in/pallas_call | solution.py:372
  95.3 3.7 %all-to-all-start.3 = ((bf16[8,64,768]{2,1,0:T(8,128)(2,1)}), bf16[8,64,768]{2,1,0:T(8,128)(2,1)S(1)}, u32[]{:S(2)}, u32[]{:S(2)}) async-start(bf16[8,64,768]{2,1,0:T(8,128)(2,1)} %bitcast.185), calls=%async_computation.3 | async-start | bytes 1572864 | tf_op jit(solution)/shard_map/all_to_all | solution.py:724
  101.5 18.1 %all-to-all-done.3 = bf16[8,64,768]{2,1,0:T(8,128)(2,1)S(1)} async-done(((bf16[8,64,768]{2,1,0:T(8,128)(2,1)}), bf16[8,64,768]{2,1,0:T(8,128)(2,1)S(1)}, u32[]{:S(2)}, u32[]{:S(2)}) %all-to-all-start.3) | async-done | bytes 786464 | tf_op jit(solution)/shard_map/all_to_all | solution.py:724
  120.4 19.2 %expert_layer.1 = (bf16[512,3072]{1,0:T(8,128)(2,1)}, bf16[512,3072]{1,0:T(8,128)(2,1)}, bf16[512,768]{1,0:T(8,128)(2,1)}, bf16[512,768]{1,0:T(8,128)(2,1)}, bf1...) custom-call(s32[5]{0:T(128)} %stack.101.own_ref, bf16[512,768]{1,0:T(8,128)(2,1)} %bitcast.159, bf16[512,896]{1,0:T(8,128)(2,1)} %bitcast.172, ...), custom_call_target="tpu_custom_call" | custom-call | bytes 170000 | tf_op jit(solution)/shard_map/expert_layer/pallas_call | solution.py:464
  139.6 3.3 %convolution_convert_fusion = bf16[768,768]{1,0:T(8,128)(2,1)} fusion(bf16[512,768]{1,0:T(8,128)(2,1)} %get-tuple-element.107, bf16[512,3072]{1,0:T(8,128)(2,1)} %get-tuple-element.153), kind=kOutput, calls=%fused_computation.6 | convolution fusion | flops 604569600 | bytes 2752512 | tf_op jit(solution)/shard_map/dot_general | solution.py:30
  142.9 3.6 %all-to-all-start.4 = ((bf16[8,64,768]{2,1,0:T(8,128)(2,1)}), bf16[8,64,768]{2,1,0:T(8,128)(2,1)S(1)}, u32[]{:S(2)}, u32[]{:S(2)}) async-start(bf16[8,64,768]{2,1,0:T(8,128)(2,1)} %bitcast.40), calls=%async_computation.4 | async-start | bytes 1572864 | tf_op jit(solution)/shard_map/all_to_all | solution.py:724
  146.6 3.1 %convolution_convert_fusion.1 = bf16[768,768]{1,0:T(8,128)(2,1)} fusion(bf16[512,768]{1,0:T(8,128)(2,1)S(1)} %bitcast.160, bf16[512,3072]{1,0:T(8,128)(2,1)} %get-tuple-element.150), kind=kOutput, calls=%fused_computation.7 | convolution fusion | flops 604569600 | bytes 2752512 | tf_op jit(solution)/shard_map/dot_general | solution.py:30
  155.0 3.1 %add_convert_fusion = bf16[768,768]{1,0:T(8,128)(2,1)} fusion(bf16[768,768]{1,0:T(8,128)(2,1)} %collective-permute-done.8, bf16[512,768]{1,0:T(8,128)(2,1)S(1)} %copy-done.16, bf16[512,3072]{1,0:T(8,128)(2,1)S(1)} %copy-done.23), kind=kOutput, calls=%fused_computation.2 | convolution fusion | flops 605749248 | bytes 3932160 | tf_op jit(solution)/shard_map/dot_general | solution.py:30
  158.5 9.1 %all-to-all-done.4 = bf16[8,64,768]{2,1,0:T(8,128)(2,1)S(1)} async-done(((bf16[8,64,768]{2,1,0:T(8,128)(2,1)}), bf16[8,64,768]{2,1,0:T(8,128)(2,1)S(1)}, u32[]{:S(2)}, u32[]{:S(2)}) %all-to-all-start.4) | async-done | bytes 786464 | tf_op jit(solution)/shard_map/all_to_all | solution.py:724
  168.4 3.4 %mlp_back.1 = (f32[128,768]{1,0:T(8,128)}, bf16[128,768]{1,0:T(8,128)(2,1)}, f32[1,768]{1,0:T(1,128)}, bf16[4,192,128]{2,1,0:T(8,128)(2,1)}) custom-call(bf16[512,768]{1,0:T(8,128)(2,1)} %bitcast.176, bf16[512,128]{1,0:T(8,128)(2,1)} %get-tuple-element.168.disp_ref, f32[128,768]{1,0:T(8,128)} %get-tuple-element.101.resid_ref, f32[128,768]{1,0:T(8,128)} %bitcast.181, ...), custom_call_target="tpu_custom_call" | custom-call | bytes 13600000 | tf_op jit(solution)/shard_map/mlp_back/pallas_call | solution.py:524
  171.7 3.4 %all-to-all-start.5 = ((bf16[4,192,128]{2,1,0:T(8,128)(2,1)}), bf16[4,192,128]{2,1,0:T(8,128)(2,1)S(1)}, u32[]{:S(2)}, u32[]{:S(2)}) async-start(bf16[4,192,128]{2,1,0:T(8,128)(2,1)} %get-tuple-element.110), calls=%async_computation.5 | async-start | bytes 393216 | tf_op jit(solution)/shard_map/all_to_all | solution.py:724
  178.1 3.2 %side_grad.1 = f32[8,96,896]{2,1,0:T(8,128)} custom-call(bf16[4,192,128]{2,1,0:T(8,128)(2,1)} %copy-done.10, bf16[128,768]{1,0:T(8,128)(2,1)} %get-tuple-element.112.grad_ref, f32[768,128]{1,0:T(8,128)} %get-tuple-element.113.router_ref), custom_call_target="tpu_custom_call" | custom-call | bytes 170000 | tf_op jit(solution)/shard_map/side_grad/pallas_call | solution.py:611
  182.6 4.6 %all-to-all-start.6 = ((bf16[8,64,768]{2,1,0:T(8,128)(2,1)}), bf16[8,64,768]{2,1,0:T(8,128)(2,1)S(1)}, u32[]{:S(2)}, u32[]{:S(2)}) async-start(bf16[8,64,768]{2,1,0:T(8,128)(2,1)} %bitcast.47), calls=%async_computation.6 | async-start | bytes 1572864 | tf_op jit(solution)/shard_map/all_to_all | solution.py:724
  189.8 9.4 %attention_backward.2 = (f32[4,128,192]{2,1,0:T(8,128)}, bf16[1,4,128,384]{3,2,1,0:T(8,128)(2,1)}, f32[1,3,5,256]{3,2,1,0:T(8,128)}) custom-call(s32[4]{0:T(128)} %get-tuple-element.171.place_ref, bf16[4,128,192]{2,1,0:T(8,128)(2,1)} %get-tuple-element.91.q_ref, bf16[1,4,128,384]{3,2,1,0:T(8,128)(2,1)} %bitcast.183, s32[4,128,1]{2,1,0:T(8,128)} %copy.52.refs_2_.start_ref, ...), custom_call_target="tpu_custom_call" | custom-call | bytes 27200000 | tf_op jit(solution)/shard_map/attention_backward/pallas_call | solution.py:313
  204.1 9.5 %attention_backward.3 = (f32[4,128,192]{2,1,0:T(8,128)}, f32[1,4,128,384]{3,2,1,0:T(8,128)}, f32[1,3,5,256]{3,2,1,0:T(8,128)}) custom-call(s32[4]{0:T(128)} %get-tuple-element.170.place_ref, bf16[4,128,192]{2,1,0:T(8,128)(2,1)} %get-tuple-element.91.q_ref, bf16[1,4,128,384]{3,2,1,0:T(8,128)(2,1)} %bitcast.182, s32[4,128,1]{2,1,0:T(8,128)} %copy.52.refs_2_.start_ref, ...), custom_call_target="tpu_custom_call" | custom-call | bytes 3400000 | tf_op jit(solution)/shard_map/attention_backward/pallas_call | solution.py:313
  213.6 3.8 %collective-permute-done.11 = bf16[768,768]{1,0:T(8,128)(2,1)} collective-permute-done((bf16[768,768]{1,0:T(8,128)(2,1)}, bf16[768,768]{1,0:T(8,128)(2,1)}, u32[]{:S(2)}, u32[]{:S(2)}) %collective-permute-start.11) | collective-permute-done | bytes 1179680 | tf_op jit(solution)/shard_map/ppermute | solution.py:707
  219.3 4.5 %project_back.1 = (bf16[512,576]{1,0:T(8,128)(2,1)}, f32[1,768]{1,0:T(1,128)}, bf16[4,128,768]{2,1,0:T(8,128)(2,1)}) custom-call(f32[4,128,192]{2,1,0:T(8,128)} %get-tuple-element.127.dq_ref, f32[4,128,192]{2,1,0:T(8,128)} %get-tuple-element.128.dq_other_ref, f32[4,128,384]{2,1,0:T(8,128)} %bitcast.186, bf16[4,128,384]{2,1,0:T(8,128)(2,1)} %copy-done.19, ...), custom_call_target="tpu_custom_call" | custom-call | bytes 13600000 | tf_op jit(solution)/shard_map/project_back/pallas_call | solution.py:566
  223.8 3.4 %qkv_grad.1 = f32[8,96,576]{2,1,0:T(8,128)} custom-call(bf16[4,128,768]{2,1,0:T(8,128)(2,1)} %get-tuple-element.126.h_ref, bf16[512,576]{1,0:T(8,128)(2,1)} %get-tuple-element.131.dproj_ref), custom_call_target="tpu_custom_call" | custom-call | bytes 170000 | tf_op jit(solution)/shard_map/qkv_grad/pallas_call | solution.py:589
  229.4 5.1 %all-to-all-start.7 = ((bf16[4,128,768]{2,1,0:T(8,128)(2,1)}), bf16[4,128,768]{2,1,0:T(8,128)(2,1)S(1)}, u32[]{:S(2)}, u32[]{:S(2)}) async-start(bf16[4,128,768]{2,1,0:T(8,128)(2,1)} %get-tuple-element.143), calls=%async_computation.7 | async-start | bytes 1572864 | tf_op jit(solution)/shard_map/all_to_all | solution.py:724
  244.2 5.7 %collective-permute-done.15 = bf16[8,24,576]{2,1,0:T(8,128)(2,1)S(1)} collective-permute-done((bf16[8,24,576]{2,1,0:T(8,128)(2,1)S(1)}, bf16[8,24,576]{2,1,0:T(8,128)(2,1)S(1)}, u32[]{:S(2)}, u32[]{:S(2)}) %collective-permute-start.15) | collective-permute-done | bytes 221216 | tf_op jit(solution)/shard_map/ppermute | solution.py:707
  252.7 3.4 %add_bitcast_fusion = f32[1,768,768]{2,1,0:T(8,128)} fusion(bf16[768,768]{1,0:T(8,128)(2,1)} %collective-permute-done.9, f32[768,768]{1,0:T(8,128)S(1)} %fusion.3, bf16[768,768]{1,0:T(8,128)(2,1)} %collective-permute-done.16), kind=kLoop, calls=%fused_computation | loop fusion | flops 2359296 | bytes 7077888 | tf_op jit(solution)/shard_map/broadcast_in_dim | solution.py:997
  256.2 3.3 %fusion.5 = f32[768,768]{1,0:T(8,128)} fusion(bf16[512,768]{1,0:T(8,128)(2,1)S(1)} %bitcast.163, bf16[512,3072]{1,0:T(8,128)(2,1)} %get-tuple-element.150), kind=kOutput, calls=%fused_computation.26 | convolution fusion | flops 603979776 | bytes 3932160 | tf_op jit(solution)/shard_map/dot_general | solution.py:30
  266.3 4.0 %add_bitcast_fusion.1 = f32[1,768,768]{2,1,0:T(8,128)} fusion(bf16[768,768]{1,0:T(8,128)(2,1)} %collective-permute-done.11, f32[768,768]{1,0:T(8,128)} %fusion.5, bf16[768,768]{1,0:T(8,128)(2,1)} %collective-permute-done.17), kind=kLoop, calls=%fused_computation.1 | loop fusion | flops 2359296 | bytes 7077888 | tf_op jit(solution)/shard_map/broadcast_in_dim | solution.py:996
  274.9 3.6 %collective-permute-done.23 = bf16[24,3456]{1,0:T(8,128)(2,1)S(1)} collective-permute-done((bf16[24,3456]{1,0:T(8,128)(2,1)}, bf16[24,3456]{1,0:T(8,128)(2,1)S(1)}, u32[]{:S(2)}, u32[]{:S(2)}) %collective-permute-start.23) | collective-permute-done | bytes 165920 | tf_op jit(solution)/shard_map/ppermute | solution.py:707
  (218 shorter events, 90.7 us)
Async XLA Ops:
  3.0 20.8 %collective-permute-start = (bf16[128,768]{1,0:T(8,128)(2,1)S(1)}, bf16[128,768]{1,0:T(8,128)(2,1)S(1)}, u32[]{:S(2)}, u32[]{:S(2)}) collective-permute-start(bf16[128,768]{1,0:T(8,128)(2,1)S(1)} %multiply_convert_fusion.h0_ref), channel_id=1, source_target_pairs={{0,2},{2,4},{4,6},{6,0},{1,3},{3,5},{5,7},{7,1},{8,10},{10,12},{12... | collective-permute-start | bytes 589832 | tf_op jit(solution)/shard_map/ppermute | solution.py:715
  6.1 17.7 %collective-permute-start.1 = (bf16[128,768]{1,0:T(8,128)(2,1)S(1)}, bf16[128,768]{1,0:T(8,128)(2,1)S(1)}, u32[]{:S(2)}, u32[]{:S(2)}) collective-permute-start(bf16[128,768]{1,0:T(8,128)(2,1)S(1)} %multiply_convert_fusion.h0_ref), channel_id=1, source_target_pairs={{0,4},{2,6},{4,0},{6,2},{1,5},{3,7},{5,1},{7,3},{8,12},{10,14},{12... | collective-permute-start | bytes 589832 | tf_op jit(solution)/shard_map/ppermute | solution.py:715
  8.7 15.1 %collective-permute-start.2 = (bf16[128,768]{1,0:T(8,128)(2,1)S(1)}, bf16[128,768]{1,0:T(8,128)(2,1)S(1)}, u32[]{:S(2)}, u32[]{:S(2)}) collective-permute-start(bf16[128,768]{1,0:T(8,128)(2,1)S(1)} %multiply_convert_fusion.h0_ref), channel_id=1, source_target_pairs={{0,6},{2,0},{4,2},{6,4},{1,7},{3,1},{5,3},{7,5},{8,14},{10,8},{12,... | collective-permute-start | bytes 589832 | tf_op jit(solution)/shard_map/ppermute | solution.py:715
  12.2 24.1 %all-to-all-start = ((bf16[8,48,576]{2,1,0:T(8,128)(2,1)}), bf16[8,48,576]{2,1,0:T(8,128)(2,1)S(1)}, u32[]{:S(2)}, u32[]{:S(2)}) async-start(bf16[8,48,576]{2,1,0:T(8,128)(2,1)} %reshape.157), calls=%async_computation | async-start | bytes 983040 | tf_op jit(solution)/shard_map/all_to_all | solution.py:724
  36.3 37.1 %all-to-all-start.1 = ((bf16[8,88,896]{2,1,0:T(8,128)(2,1)}), bf16[8,88,896]{2,1,0:T(8,128)(2,1)S(1)}, u32[]{:S(2)}, u32[]{:S(2)}) async-start(bf16[8,88,896]{2,1,0:T(8,128)(2,1)} %pad_maximum_fusion), calls=%async_computation.1 | async-start | bytes 2523136 | tf_op jit(solution)/shard_map/all_to_all | solution.py:724
  40.1 1.9 collective-permute-start.3
  46.8 18.6 %collective-permute-start.4 = (bf16[4,128,384]{2,1,0:T(8,128)(2,1)}, bf16[4,128,384]{2,1,0:T(8,128)(2,1)S(1)}, u32[]{:S(2)}, u32[]{:S(2)}) collective-permute-start(bf16[4,128,384]{2,1,0:T(8,128)(2,1)} %get-tuple-element.92.refs_0_), channel_id=1, source_target_pairs={{0,1},{1,0},{2,3},{3,2},{4,5},{5,4},{6,7},{7,6},{8,9},{9,8},{10,11... | collective-permute-start | bytes 1179656 | tf_op jit(solution)/shard_map/ppermute | solution.py:707
  73.4 10.0 %collective-permute-start.5 = (bf16[8,24,896]{2,1,0:T(8,128)(2,1)S(1)}, bf16[8,24,896]{2,1,0:T(8,128)(2,1)S(1)}, u32[]{:S(2)}, u32[]{:S(2)}) collective-permute-start(bf16[8,24,896]{2,1,0:T(8,128)(2,1)S(1)} %get-tuple-element.157), channel_id=1, source_target_pairs={{0,16},{16,0},{1,17},{17,1},{2,18},{18,2},{3,19},{19,3},{4,20},{20... | collective-permute-start | bytes 1032200 | tf_op jit(solution)/shard_map/ppermute | solution.py:707
  75.0 13.6 %all-to-all-start.2 = ((bf16[4,192,128]{2,1,0:T(8,128)(2,1)}), bf16[4,192,128]{2,1,0:T(8,128)(2,1)S(1)}, u32[]{:S(2)}, u32[]{:S(2)}) async-start(bf16[4,192,128]{2,1,0:T(8,128)(2,1)} %get-tuple-element.97), calls=%async_computation.2 | async-start | bytes 393216 | tf_op jit(solution)/shard_map/all_to_all | solution.py:724
  88.6 2.1 collective-permute-start.6
  95.3 24.2 %all-to-all-start.3 = ((bf16[8,64,768]{2,1,0:T(8,128)(2,1)}), bf16[8,64,768]{2,1,0:T(8,128)(2,1)S(1)}, u32[]{:S(2)}, u32[]{:S(2)}) async-start(bf16[8,64,768]{2,1,0:T(8,128)(2,1)} %bitcast.185), calls=%async_computation.3 | async-start | bytes 1572864 | tf_op jit(solution)/shard_map/all_to_all | solution.py:724
  142.9 12.1 %collective-permute-start.8 = (bf16[768,768]{1,0:T(8,128)(2,1)}, bf16[768,768]{1,0:T(8,128)(2,1)}, u32[]{:S(2)}, u32[]{:S(2)}) collective-permute-start(bf16[768,768]{1,0:T(8,128)(2,1)} %convolution_convert_fusion), channel_id=1, source_target_pairs={{0,8},{8,0},{1,9},{9,1},{2,10},{10,2},{3,11},{11,3},{4,12},{12,4},... | collective-permute-start | bytes 3538952 | tf_op jit(solution)/shard_map/ppermute | solution.py:707
  142.9 24.6 %all-to-all-start.4 = ((bf16[8,64,768]{2,1,0:T(8,128)(2,1)}), bf16[8,64,768]{2,1,0:T(8,128)(2,1)S(1)}, u32[]{:S(2)}, u32[]{:S(2)}) async-start(bf16[8,64,768]{2,1,0:T(8,128)(2,1)} %bitcast.40), calls=%async_computation.4 | async-start | bytes 1572864 | tf_op jit(solution)/shard_map/all_to_all | solution.py:724
  149.7 25.4 %collective-permute-start.7 = (bf16[768,768]{1,0:T(8,128)(2,1)}, bf16[768,768]{1,0:T(8,128)(2,1)S(1)}, u32[]{:S(2)}, u32[]{:S(2)}) collective-permute-start(bf16[768,768]{1,0:T(8,128)(2,1)} %convolution_convert_fusion.1), channel_id=1, source_target_pairs={{0,8},{8,0},{1,9},{9,1},{2,10},{10,2},{3,11},{11,3},{4,12},{12,4},... | collective-permute-start | bytes 3538952 | tf_op jit(solution)/shard_map/ppermute | solution.py:707
  158.1 42.8 %collective-permute-start.9 = (bf16[768,768]{1,0:T(8,128)(2,1)}, bf16[768,768]{1,0:T(8,128)(2,1)}, u32[]{:S(2)}, u32[]{:S(2)}) collective-permute-start(bf16[768,768]{1,0:T(8,128)(2,1)} %add_convert_fusion), channel_id=1, source_target_pairs={{0,16},{16,0},{1,17},{17,1},{2,18},{18,2},{3,19},{19,3},{4,20},{20... | collective-permute-start | bytes 3538952 | tf_op jit(solution)/shard_map/ppermute | solution.py:707
  171.7 10.8 %all-to-all-start.5 = ((bf16[4,192,128]{2,1,0:T(8,128)(2,1)}), bf16[4,192,128]{2,1,0:T(8,128)(2,1)S(1)}, u32[]{:S(2)}, u32[]{:S(2)}) async-start(bf16[4,192,128]{2,1,0:T(8,128)(2,1)} %get-tuple-element.110), calls=%async_computation.5 | async-start | bytes 393216 | tf_op jit(solution)/shard_map/all_to_all | solution.py:724
  182.6 34.8 %all-to-all-start.6 = ((bf16[8,64,768]{2,1,0:T(8,128)(2,1)}), bf16[8,64,768]{2,1,0:T(8,128)(2,1)S(1)}, u32[]{:S(2)}, u32[]{:S(2)}) async-start(bf16[8,64,768]{2,1,0:T(8,128)(2,1)} %bitcast.47), calls=%async_computation.6 | async-start | bytes 1572864 | tf_op jit(solution)/shard_map/all_to_all | solution.py:724
  188.6 10.5 %collective-permute-start.10 = (bf16[8,48,896]{2,1,0:T(8,128)(2,1)S(1)}, bf16[8,48,896]{2,1,0:T(8,128)(2,1)}, u32[]{:S(2)}, u32[]{:S(2)}) collective-permute-start(bf16[8,48,896]{2,1,0:T(8,128)(2,1)S(1)} %fusion.19), channel_id=1, source_target_pairs={{0,8},{8,0},{1,9},{9,1},{2,10},{10,2},{3,11},{11,3},{4,12},{12,4},... | collective-permute-start | bytes 2064392 | tf_op jit(solution)/shard_map/ppermute | solution.py:707
  188.7 28.7 %collective-permute-start.11 = (bf16[768,768]{1,0:T(8,128)(2,1)}, bf16[768,768]{1,0:T(8,128)(2,1)}, u32[]{:S(2)}, u32[]{:S(2)}) collective-permute-start(bf16[768,768]{1,0:T(8,128)(2,1)} %add_convert_fusion.1), channel_id=1, source_target_pairs={{0,16},{16,0},{1,17},{17,1},{2,18},{18,2},{3,19},{19,3},{4,20},{20... | collective-permute-start | bytes 3538952 | tf_op jit(solution)/shard_map/ppermute | solution.py:707
  200.9 17.7 %collective-permute-start.13 = (bf16[4,128,384]{2,1,0:T(8,128)(2,1)}, bf16[4,128,384]{2,1,0:T(8,128)(2,1)S(1)}, u32[]{:S(2)}, u32[]{:S(2)}) collective-permute-start(bf16[4,128,384]{2,1,0:T(8,128)(2,1)} %bitcast.53), channel_id=1, source_target_pairs={{0,1},{1,0},{2,3},{3,2},{4,5},{5,4},{6,7},{7,6},{8,9},{9,8},{10,11... | collective-permute-start | bytes 1179656 | tf_op jit(solution)/shard_map/ppermute | solution.py:707
  203.6 46.5 %collective-permute-start.16 = (bf16[768,768]{1,0:T(8,128)(2,1)}, bf16[768,768]{1,0:T(8,128)(2,1)}, u32[]{:S(2)}, u32[]{:S(2)}) collective-permute-start(bf16[768,768]{1,0:T(8,128)(2,1)} %convolution_convert_fusion.3), channel_id=1, source_target_pairs={{0,8},{8,0},{1,9},{9,1},{2,10},{10,2},{3,11},{11,3},{4,12},{12,4},... | collective-permute-start | bytes 3538952 | tf_op jit(solution)/shard_map/ppermute | solution.py:707
  203.6 46.5 %collective-permute-start.17 = (bf16[768,768]{1,0:T(8,128)(2,1)}, bf16[768,768]{1,0:T(8,128)(2,1)}, u32[]{:S(2)}, u32[]{:S(2)}) collective-permute-start(bf16[768,768]{1,0:T(8,128)(2,1)} %convolution_convert_fusion.2), channel_id=1, source_target_pairs={{0,8},{8,0},{1,9},{9,1},{2,10},{10,2},{3,11},{11,3},{4,12},{12,4},... | collective-permute-start | bytes 3538952 | tf_op jit(solution)/shard_map/ppermute | solution.py:707
  218.2 18.6 %collective-permute-start.12 = (bf16[8,24,896]{2,1,0:T(8,128)(2,1)}, bf16[8,24,896]{2,1,0:T(8,128)(2,1)}, u32[]{:S(2)}, u32[]{:S(2)}) collective-permute-start(bf16[8,24,896]{2,1,0:T(8,128)(2,1)} %fusion.22), channel_id=1, source_target_pairs={{0,16},{16,0},{1,17},{17,1},{2,18},{18,2},{3,19},{19,3},{4,20},{20... | collective-permute-start | bytes 1032200 | tf_op jit(solution)/shard_map/ppermute | solution.py:707
  229.4 9.4 %collective-permute-start.14 = (bf16[8,48,576]{2,1,0:T(8,128)(2,1)}, bf16[8,48,576]{2,1,0:T(8,128)(2,1)}, u32[]{:S(2)}, u32[]{:S(2)}) collective-permute-start(bf16[8,48,576]{2,1,0:T(8,128)(2,1)} %fusion.21), channel_id=1, source_target_pairs={{0,8},{8,0},{1,9},{9,1},{2,10},{10,2},{3,11},{11,3},{4,12},{12,4},... | collective-permute-start | bytes 1327112 | tf_op jit(solution)/shard_map/ppermute | solution.py:707
  229.4 31.0 %all-to-all-start.7 = ((bf16[4,128,768]{2,1,0:T(8,128)(2,1)}), bf16[4,128,768]{2,1,0:T(8,128)(2,1)S(1)}, u32[]{:S(2)}, u32[]{:S(2)}) async-start(bf16[4,128,768]{2,1,0:T(8,128)(2,1)} %get-tuple-element.143), calls=%async_computation.7 | async-start | bytes 1572864 | tf_op jit(solution)/shard_map/all_to_all | solution.py:724
  240.4 3.8 %collective-permute-start.19 = (f32[24,128]{1,0:T(8,128)S(1)}, f32[24,128]{1,0:T(8,128)S(1)}, u32[]{:S(2)}, u32[]{:S(2)}) collective-permute-start(f32[24,128]{1,0:T(8,128)S(1)} %pad.28), channel_id=1, source_target_pairs={{0,1},{1,0},{2,3},{3,2},{4,5},{5,4},{6,7},{7,6},{8,9},{9,8},{10,11... | collective-permute-start | bytes 36872 | tf_op jit(solution)/shard_map/ppermute | solution.py:707
  242.0 7.9 %collective-permute-start.15 = (bf16[8,24,576]{2,1,0:T(8,128)(2,1)S(1)}, bf16[8,24,576]{2,1,0:T(8,128)(2,1)S(1)}, u32[]{:S(2)}, u32[]{:S(2)}) collective-permute-start(bf16[8,24,576]{2,1,0:T(8,128)(2,1)S(1)} %fusion.27), channel_id=1, source_target_pairs={{0,16},{16,0},{1,17},{17,1},{2,18},{18,2},{3,19},{19,3},{4,20},{20... | collective-permute-start | bytes 663560 | tf_op jit(solution)/shard_map/ppermute | solution.py:707
  252.1 8.1 %collective-permute-start.18 = (bf16[4,24,1472]{2,1,0:T(8,128)(2,1)S(1)}, bf16[4,24,1472]{2,1,0:T(8,128)(2,1)S(1)}, u32[]{:S(2)}, u32[]{:S(2)}) collective-permute-start(bf16[4,24,1472]{2,1,0:T(8,128)(2,1)S(1)} %fusion.23), channel_id=1, source_target_pairs={{0,1},{1,0},{2,3},{3,2},{4,5},{5,4},{6,7},{7,6},{8,9},{9,8},{10,11... | collective-permute-start | bytes 847880 | tf_op jit(solution)/shard_map/ppermute | solution.py:707
  261.0 9.3 %collective-permute-start.20 = (bf16[24,1728]{1,0:T(8,128)(2,1)S(1)}, bf16[24,1728]{1,0:T(8,128)(2,1)S(1)}, u32[]{:S(2)}, u32[]{:S(2)}) collective-permute-start(bf16[24,1728]{1,0:T(8,128)(2,1)S(1)} %get-tuple-element.160), channel_id=1, source_target_pairs={{0,2},{2,4},{4,6},{6,0},{1,3},{3,5},{5,7},{7,1},{8,10},{10,12},{12... | collective-permute-start | bytes 248840 | tf_op jit(solution)/shard_map/ppermute | solution.py:715
  262.5 7.9 %collective-permute-start.21 = (bf16[24,1728]{1,0:T(8,128)(2,1)S(1)}, bf16[24,1728]{1,0:T(8,128)(2,1)S(1)}, u32[]{:S(2)}, u32[]{:S(2)}) collective-permute-start(bf16[24,1728]{1,0:T(8,128)(2,1)S(1)} %get-tuple-element.159), channel_id=1, source_target_pairs={{0,4},{2,6},{4,0},{6,2},{1,5},{3,7},{5,1},{7,3},{8,12},{10,14},{12... | collective-permute-start | bytes 248840 | tf_op jit(solution)/shard_map/ppermute | solution.py:715
  264.8 5.6 %collective-permute-start.22 = (bf16[24,1728]{1,0:T(8,128)(2,1)S(1)}, bf16[24,1728]{1,0:T(8,128)(2,1)S(1)}, u32[]{:S(2)}, u32[]{:S(2)}) collective-permute-start(bf16[24,1728]{1,0:T(8,128)(2,1)S(1)} %get-tuple-element.158), channel_id=1, source_target_pairs={{0,6},{2,0},{4,2},{6,4},{1,7},{3,1},{5,3},{7,5},{8,14},{10,8},{12,... | collective-permute-start | bytes 248840 | tf_op jit(solution)/shard_map/ppermute | solution.py:715
  272.9 5.6 %collective-permute-start.23 = (bf16[24,3456]{1,0:T(8,128)(2,1)}, bf16[24,3456]{1,0:T(8,128)(2,1)S(1)}, u32[]{:S(2)}, u32[]{:S(2)}) collective-permute-start(bf16[24,3456]{1,0:T(8,128)(2,1)} %assemble.1), channel_id=1, source_target_pairs={{0,16},{16,0},{1,17},{17,1},{2,18},{18,2},{3,19},{19,3},{4,20},{20... | collective-permute-start | bytes 497672 | tf_op jit(solution)/shard_map/ppermute | solution.py:707
  (41 other events, 254.3 us)
